TPU v7x, 32 devices: a whole 2x2x4 slice. The times are simulated.
32 devices in a mesh: gz: 4 (over y, core), xy: 8 (over z, x).
Axes of the slice: x: 2, y: 2, z: 4, core: 2. Of those that a mesh axis runs over, the one named last changes fastest.
Arguments:
- volume: bfloat16 [32, 64, 2048], P('gz', 'xy'), may hold values from -6 to 6
- backbone_weight: bfloat16 [64, 1728], replicated, may hold values from -0.15625 to 0.15625
- refine_weight: bfloat16 [64, 1728], replicated, may hold values from -0.15625 to 0.15625
- mix_weight: bfloat16 [64, 64], replicated, may hold values from -0.75 to 0.75
- tile_cot: bfloat16 [4, 8, 8, 2, 8, 8, 512], P('gz', 'xy'), may hold values from -6 to 6
- tile_slot: int32 [4, 8, 8, 2], P('gz', 'xy'), may hold values from 0 to 3
- tile_count: int32 [4, 8, 8], P('gz'), may hold values from 0 to 2, as said below
Outputs:
- volume_grad: bfloat16 [32, 64, 2048], P('gz', 'xy')
- backbone_step: float32 [64, 1728], replicated
- refine_step: float32 [64, 1728], replicated
- mix_step: float32 [64, 64], replicated
Inputs may be any that keep to these rules, and one draw needn't show every extreme that they name: `tile_count`: in every slab each owner receives exactly 8 live slots in all; some pairs of brick and owner use all 2 slots. `tile_slot`: only slots j < tile_count[g, s, d] are read.
All inputs are finite; a program needn't handle non-finite values.
Results may differ from a plain program's by a relative error of at most 0.0059.
Values may be sent and summed in bfloat16 or wider, within the bound.
A program may use at most 192 MiB of HBM per device.

v0:
```python
import functools

import jax
import jax.numpy as jnp
from jax import lax
from jax.experimental import pallas as pl
from jax.experimental.pallas import tpu as pltpu
from jax.sharding import PartitionSpec as P

EPSILON = 1e-06
F32 = jnp.float32
BF16 = jnp.bfloat16
VMEM = pl.BlockSpec(memory_space=pltpu.VMEM)


def neighbours():
    return [(dz, dy) for dz in (-1, 0, 1) for dy in (-1, 0, 1) if (dz, dy) != (0, 0)]


def rim_kernel(n_gz, n_xy, block, framed, send, recv):
    depth, rows = block.shape[0], block.shape[1]
    gz, xy = lax.axis_index("gz"), lax.axis_index("xy")
    framed[...] = jnp.zeros_like(framed)
    framed[pl.ds(1, depth), pl.ds(1, rows)] = block[...]

    def there(dz, dy):
        inside = (gz + dz >= 0) & (gz + dz < n_gz) & (xy + dy >= 0) & (xy + dy < n_xy)
        return inside, (gz + dz, xy + dy)

    def span(step, size, far):
        if step == 0:
            return pl.ds(1, size) if far else pl.ds(0, size)
        if far:
            return pl.ds(0, 1) if step > 0 else pl.ds(size + 1, 1)
        return pl.ds(size - 1, 1) if step > 0 else pl.ds(0, 1)

    def copy(dz, dy, number):
        _, where = there(dz, dy)
        return pltpu.make_async_remote_copy(
            src_ref=block.at[span(dz, depth, False), span(dy, rows, False)],
            dst_ref=framed.at[span(dz, depth, True), span(dy, rows, True)],
            send_sem=send.at[number],
            recv_sem=recv.at[number],
            device_id=where,
            device_id_type=pl.DeviceIdType.MESH,
        )

    barrier = pltpu.get_barrier_semaphore()
    for dz, dy in neighbours():
        inside, where = there(dz, dy)

        @pl.when(inside)
        def _():
            pl.semaphore_signal(
                barrier, inc=1, device_id=where, device_id_type=pl.DeviceIdType.MESH
            )

    across = 1 + lax.min(gz, 1) + lax.min(n_gz - 1 - gz, 1)
    along = 1 + lax.min(xy, 1) + lax.min(n_xy - 1 - xy, 1)
    pl.semaphore_wait(barrier, across * along - 1)

    for number, (dz, dy) in enumerate(neighbours()):

        @pl.when(there(dz, dy)[0])
        def _():
            copy(dz, dy, number).start()

    for number, (dz, dy) in enumerate(neighbours()):

        @pl.when(there(dz, dy)[0])
        def _():
            copy(dz, dy, number).wait_send()

        @pl.when(there(-dz, -dy)[0])
        def _():
            copy(dz, dy, number).wait_recv()


def with_rims(block, collective_id, n_gz, n_xy):
    depth, rows, pairs, lanes = block.shape
    return pl.pallas_call(
        functools.partial(rim_kernel, n_gz, n_xy),
        out_shape=jax.ShapeDtypeStruct((depth + 2, rows + 2, pairs, lanes), block.dtype),
        in_specs=[VMEM],
        out_specs=VMEM,
        scratch_shapes=[pltpu.SemaphoreType.DMA((8,))] * 2,
        compiler_params=pltpu.CompilerParams(collective_id=collective_id, has_side_effects=True),
    )(block)


def weight_halves(weight, half, turned):
    lows, highs = [], []
    count = weight.shape[1] // half
    for first in range(0, count, 2):
        if first + 1 < count:
            near = weight[:, pl.ds(first * half, 2 * half)].astype(F32)
        else:
            last = weight[:, pl.ds(first * half, half)].astype(F32)
            near = jnp.concatenate([last, jnp.zeros_like(last)], axis=1)
        far = pltpu.roll(near, half, 1)
        if turned:
            both = jnp.concatenate([near, far], axis=0).T
            near, far = both[:half], both[half:]
        lows += [near, far]
        highs += [far, near]
    return lows, highs


def fill_band(target, weight, turned):
    half = weight.shape[0]
    lows, highs = weight_halves(weight, half, turned)
    low = lax.broadcasted_iota(jnp.int32, (half, 2 * half), 1) < half
    for offset in range(9):
        ks = [26 - 3 * offset - x if turned else 3 * offset + x for x in range(3)]
        parts = [
            jnp.where(low, lows[ks[1]], highs[ks[0]]),
            jnp.where(low, lows[ks[2]], highs[ks[1]]),
            jnp.where(low, 0.0, highs[ks[2]]),
            jnp.where(low, lows[ks[0]], 0.0),
        ]
        for place, part in enumerate(parts):
            target[pl.ds((4 * offset + place) * half, half), :] = part.astype(BF16)


def side_lanes(cells, half, period):
    pairs = cells.shape[1]
    lane = lax.broadcasted_iota(jnp.int32, cells.shape, 2)
    place = lax.broadcasted_iota(jnp.int32, cells.shape, 1) % period
    right = pltpu.roll(cells, pairs - 1, 1)
    left = pltpu.roll(cells, 1, 1)
    low = lane < half
    right = jnp.where(place == period - 1, 0.0, right)
    left = jnp.where(place == 0, 0.0, left)
    return jnp.where(low, right, left)


def fill_windows(target, source, half, period, inner):
    depth = target.shape[0]
    lanes = 2 * half
    if inner:
        target[...] = jnp.zeros_like(target)
    first, last = (1, depth - 1) if inner else (0, depth)
    for z in range(first, last):
        cells = source(z - first)
        rows = pl.ds(1, target.shape[1] - 2) if inner else pl.ds(0, target.shape[1])
        target[z, rows, :, pl.ds(0, lanes)] = cells.astype(BF16)
        target[z, rows, :, pl.ds(lanes, lanes)] = side_lanes(cells.astype(F32), half, period).astype(
            BF16
        )


def window_rows(windows, z, count, dz, dy):
    rows = windows.shape[1] - 2
    pairs, width = windows.shape[2], windows.shape[3]
    part = windows[pl.ds(z + dz, count), pl.ds(dy, rows)]
    return part.reshape(count * rows * pairs, width)


def conv_rows(windows, weight, z, count):
    parts = [window_rows(windows, z, count, dz, dy) for dz in range(3) for dy in range(3)]
    return jnp.dot(jnp.concatenate(parts, axis=1), weight[...], preferred_element_type=F32)


def outer_sums(out, base, windows, grad_turned, half):
    depth = windows.shape[0] - 2
    lanes = 2 * half
    lane = lax.broadcasted_iota(jnp.int32, (half, lanes), 1)
    held = None
    for offset in range(9):
        both = jnp.dot(
            grad_turned,
            window_rows(windows, 0, depth, offset // 3, offset % 3),
            preferred_element_type=F32,
        )
        top_near, top_far = both[:half, :lanes], both[:half, lanes:]
        far_turned = pltpu.roll(top_far, half, 1)
        near_turned = pltpu.roll(top_near, half, 1)
        first = jnp.where(lane < half, far_turned, near_turned) + both[half:, :lanes]
        third = near_turned + both[half:, lanes:]
        out[pl.ds(base + offset * half, half), :] = first.astype(BF16)
        if offset % 2 == 0:
            held = jnp.where(lane < half, third, 0.0)
        else:
            pair = held + jnp.where(lane < half, 0.0, pltpu.roll(third, half, 1))
            out[pl.ds(base + (9 + offset // 2) * half, half), :] = pair.astype(BF16)
    out[pl.ds(base + 13 * half, half), :] = held.astype(BF16)


def refine_kernel(
    period, vol, cot, back, refine, mix, fgrad, rsum, msum, xw, fw, pw, wb, wr, wrt, gate_s, pg_s
):
    depth, rows, pairs, lanes = fgrad.shape
    half = lanes // 2
    step = 4 if depth % 4 == 0 else depth
    flat = step * rows * pairs
    fill_band(wb, back, False)
    fill_band(wr, refine, False)
    fill_band(wrt, refine, True)
    mixed = mix[...].astype(F32)
    mixed = jnp.concatenate([mixed, jnp.zeros_like(mixed)], axis=1)
    mix2 = jnp.concatenate([mixed, pltpu.roll(mixed, half, 1)], axis=0).T.astype(BF16)
    fill_windows(xw, lambda z: vol[z], half, pairs, False)
    fw[...] = jnp.zeros_like(fw)
    pw[...] = jnp.zeros_like(pw)
    inner = pl.ds(1, rows)

    def put(target, z, cells):
        target[pl.ds(z + 1, step), inner, :, pl.ds(0, lanes)] = cells.astype(BF16)
        near = cells.astype(F32).reshape(step * rows, pairs, lanes)
        target[pl.ds(z + 1, step), inner, :, pl.ds(lanes, lanes)] = (
            side_lanes(near, half, period).astype(BF16).reshape(step, rows, pairs, lanes)
        )

    for z in range(0, depth, step):
        own = vol[pl.ds(z + 1, step), inner].astype(F32).reshape(flat, lanes)
        feature = (own + conv_rows(xw, wb, z, step)).astype(BF16)
        put(fw, z, feature.reshape(step, rows, pairs, lanes))
    for z in range(0, depth, step):
        pre = conv_rows(fw, wr, z, step)
        sig = jax.nn.sigmoid(pre)
        total = cot[pl.ds(z, step)].reshape(flat, lanes).astype(BF16)
        gate_s[pl.ds(z * rows * pairs, flat), :] = (pre * sig).astype(BF16)
        gated_grad = jnp.dot(total, mix2, preferred_element_type=F32)
        pre_grad = (gated_grad * sig * (1.0 + pre * (1.0 - sig))).astype(BF16)
        pg_s[pl.ds(z * rows * pairs, flat), :] = pre_grad
        put(pw, z, pre_grad.reshape(step, rows, pairs, lanes))
    for z in range(0, depth, step):
        total = cot[pl.ds(z, step)].reshape(flat, lanes)
        grad = total + conv_rows(pw, wrt, z, step)
        fgrad[pl.ds(z, step)] = grad.astype(BF16).reshape(step, rows, pairs, lanes)
    outer_sums(rsum, 0, fw, pg_s[...].T, half)
    cot_rows = cot[...].reshape(depth * rows * pairs, lanes).astype(BF16)
    both = jnp.dot(gate_s[...].T, cot_rows, preferred_element_type=F32)
    lane = lax.broadcasted_iota(jnp.int32, (half, lanes), 1)
    msum[...] = jnp.where(lane < half, both[:half] + pltpu.roll(both[half:], half, 1), 0.0).astype(
        BF16
    )


def backbone_kernel(vol, grad, back, rsum, msum, vgrad, sums, xw, gw, wbt):
    depth, rows, pairs, lanes = vgrad.shape
    half = lanes // 2
    step = 4 if depth % 4 == 0 else depth
    flat = step * rows * pairs
    fill_band(wbt, back, True)
    fill_windows(xw, lambda z: vol[z], half, pairs, False)
    fill_windows(gw, lambda z: grad[z], half, pairs, False)
    inner = pl.ds(1, rows)
    for z in range(0, depth, step):
        own = grad[pl.ds(z + 1, step), inner].astype(F32).reshape(flat, lanes)
        out = own + conv_rows(gw, wbt, z, step)
        vgrad[pl.ds(z, step)] = out.astype(BF16).reshape(step, rows, pairs, lanes)
    own = grad[pl.ds(1, depth), inner].reshape(depth * rows * pairs, lanes)
    outer_sums(sums, 0, xw, own.T, half)
    block = rsum.shape[0]
    sums[pl.ds(block, block), :] = rsum[...]
    sums[pl.ds(2 * block, half), :] = msum[...]
    used = 2 * block + half
    if used < sums.shape[0]:
        sums[pl.ds(used, sums.shape[0] - used), :] = jnp.zeros(
            (sums.shape[0] - used, lanes), BF16
        )


def total_kernel(n_gz, n_xy, sums, out, got1, part, got2, mine, *sems):
    gz, xy = lax.axis_index("gz"), lax.axis_index("xy")
    chunk = mine.shape[0]
    block = part.shape[0]
    barrier = pltpu.get_barrier_semaphore()

    def peer(axis, step):
        if axis == "gz":
            target = lax.rem(gz + step, n_gz)
            return target, (target, xy)
        target = lax.rem(xy + step, n_xy)
        return target, (gz, target)

    sizes = {"gz": n_gz, "xy": n_xy}

    def each(axis, action):
        def one(step, carry):
            action(step)
            return carry

        lax.fori_loop(1, sizes[axis], one, 0)

    def greet(axis):
        def one(step):
            pl.semaphore_signal(
                barrier,
                inc=1,
                device_id=peer(axis, step)[1],
                device_id_type=pl.DeviceIdType.MESH,
            )

        each(axis, one)

    greet("gz")
    greet("xy")
    pl.semaphore_wait(barrier, n_gz + n_xy - 2)

    def copy(axis, stage, source, target):
        def make(step):
            where, device = peer(axis, step)
            return pltpu.make_async_remote_copy(
                src_ref=source(where),
                dst_ref=target(step),
                send_sem=sems[2 * stage].at[step],
                recv_sem=sems[2 * stage + 1].at[step],
                device_id=device,
                device_id_type=pl.DeviceIdType.MESH,
            )

        return make

    blocks = copy("gz", 0, lambda w: sums.at[pl.ds(w * block, block)], lambda s: got1.at[s])
    each("gz", lambda step: blocks(step).start())
    each("gz", lambda step: blocks(step).wait_recv())
    total = sums[pl.ds(gz * block, block), :].astype(F32)
    for step in range(1, n_gz):
        total = total + got1[step].astype(F32)
    part[...] = total.astype(BF16)
    chunks = copy("xy", 1, lambda w: part.at[pl.ds(w * chunk, chunk)], lambda s: got2.at[s])
    each("xy", lambda step: chunks(step).start())
    each("xy", lambda step: chunks(step).wait_recv())
    total = part[pl.ds(xy * chunk, chunk), :].astype(F32)
    for step in range(1, n_xy):
        total = total + got2[step].astype(F32)
    mine[...] = total.astype(BF16)
    own = pl.ds(gz * block + xy * chunk, chunk)
    spread = copy("xy", 2, lambda w: mine, lambda s: out.at[own])
    each("xy", lambda step: spread(step).start())
    out[own, :] = mine[...]
    each("xy", lambda step: spread(step).wait_recv())
    ours = pl.ds(gz * block, block)
    again = copy("gz", 3, lambda w: out.at[ours], lambda s: out.at[ours])
    each("gz", lambda step: again(step).start())
    each("gz", lambda step: blocks(step).wait_send())
    each("xy", lambda step: chunks(step).wait_send())
    each("xy", lambda step: spread(step).wait_send())
    each("gz", lambda step: again(step).wait())


def finish_kernel(totals, back_step, refine_step, mix_step):
    half = mix_step.shape[0]
    lanes = 2 * half
    block = 14 * half
    low = lax.broadcasted_iota(jnp.int32, (half, lanes), 1) < half

    def scale_of(values, count):
        squares = jnp.sum(values * values, axis=0, keepdims=True)
        return jnp.sqrt(jnp.sum(squares, axis=1, keepdims=True) / count + EPSILON)

    for base, out in ((0, back_step), (block, refine_step)):
        values = totals[pl.ds(base, block), :].astype(F32)
        scale = scale_of(values, 27.0 * half * half)
        lows, highs = [None] * 28, [None] * 28
        for tile in range(14):
            near = values[tile * half : (tile + 1) * half]
            both = jnp.concatenate([near, pltpu.roll(near, half, 1)], axis=0).T / scale
            if tile < 9:
                first, second = 3 * tile, 3 * tile + 1
            else:
                first, second = 6 * (tile - 9) + 2, 6 * (tile - 9) + 5
            lows[first], highs[first] = both[:half], both[half:]
            if second < 27:
                lows[second], highs[second] = both[half:], both[:half]
        for k in range(0, 26, 2):
            out[:, pl.ds(k * half, lanes)] = jnp.where(low, lows[k], highs[k + 1])
        out[:, pl.ds(26 * half, half)] = lows[26][:, :half]
    values = totals[pl.ds(2 * block, half), :].astype(F32)
    mix_step[...] = (values / scale_of(values, 1.0 * half * half))[:, :half]


def body(volume, backbone_weight, refine_weight, mix_weight, tile_cot, tile_slot, tile_count):
    depth, rows, width = volume.shape
    channels = mix_weight.shape[0]
    edge = tile_cot.shape[4]
    owners, capacity = tile_cot.shape[2], tile_cot.shape[3]
    assert depth == edge and rows == edge
    lanes = 2 * channels
    pairs = width // lanes
    period = edge // 2
    tiles = pairs // period
    slots = owners * capacity
    n_gz, n_xy = lax.axis_size("gz"), lax.axis_size("xy")
    devices = n_gz * n_xy
    brick = (depth, rows, pairs, lanes)
    rimmed = with_rims(volume.reshape(brick), 1, n_gz, n_xy)

    my_counts = jnp.sum(
        tile_count[0]
        * (jnp.arange(owners, dtype=jnp.int32) == lax.axis_index("xy")).astype(jnp.int32)[:, None],
        axis=0,
    )
    live = (jnp.arange(capacity, dtype=jnp.int32)[None, :] < my_counts[:, None]).reshape(slots)
    picker = (
        (tile_slot.reshape(slots)[None, :] == jnp.arange(tiles, dtype=jnp.int32)[:, None])
        & live[None, :]
    ).astype(BF16)
    cot = jnp.dot(
        picker, tile_cot.reshape(slots, edge * edge * edge * channels), preferred_element_type=F32
    )
    cot = cot.reshape(tiles, depth, rows, period, lanes).transpose(1, 2, 0, 3, 4).reshape(brick)

    block = 14 * channels
    framed = (depth + 2, rows + 2, pairs, 2 * lanes)
    params = pltpu.CompilerParams(vmem_limit_bytes=56 * 1024 * 1024)
    fgrad, rsum, msum = pl.pallas_call(
        functools.partial(refine_kernel, period),
        out_shape=(
            jax.ShapeDtypeStruct(brick, BF16),
            jax.ShapeDtypeStruct((block, lanes), BF16),
            jax.ShapeDtypeStruct((channels, lanes), BF16),
        ),
        in_specs=[VMEM] * 5,
        out_specs=(VMEM,) * 3,
        scratch_shapes=[
            pltpu.VMEM(framed, BF16),
            pltpu.VMEM(framed, BF16),
            pltpu.VMEM(framed, BF16),
            pltpu.VMEM((36 * channels, lanes), BF16),
            pltpu.VMEM((36 * channels, lanes), BF16),
            pltpu.VMEM((36 * channels, lanes), BF16),
            pltpu.VMEM((depth * rows * pairs, lanes), BF16),
            pltpu.VMEM((depth * rows * pairs, lanes), BF16),
        ],
        compiler_params=params,
    )(
        rimmed,
        cot,
        backbone_weight,
        refine_weight,
        mix_weight,
    )
    grad_rimmed = with_rims(fgrad, 2, n_gz, n_xy)
    used = 2 * block + channels
    chunk = -(-used // (devices * 16)) * 16
    vgrad, sums = pl.pallas_call(
        backbone_kernel,
        out_shape=(
            jax.ShapeDtypeStruct(brick, BF16),
            jax.ShapeDtypeStruct((devices * chunk, lanes), BF16),
        ),
        in_specs=[VMEM] * 5,
        out_specs=(VMEM,) * 2,
        scratch_shapes=[
            pltpu.VMEM(framed, BF16),
            pltpu.VMEM(framed, BF16),
            pltpu.VMEM((36 * channels, lanes), BF16),
        ],
        compiler_params=params,
    )(rimmed, grad_rimmed, backbone_weight, rsum, msum)
    totals = pl.pallas_call(
        functools.partial(total_kernel, n_gz, n_xy),
        out_shape=jax.ShapeDtypeStruct((devices * chunk, lanes), BF16),
        in_specs=[VMEM],
        out_specs=VMEM,
        scratch_shapes=[
            pltpu.VMEM((n_gz, n_xy * chunk, lanes), BF16),
            pltpu.VMEM((n_xy * chunk, lanes), BF16),
            pltpu.VMEM((n_xy, chunk, lanes), BF16),
            pltpu.VMEM((chunk, lanes), BF16),
        ]
        + [pltpu.SemaphoreType.DMA((n,)) for n in (n_gz, n_gz, n_xy, n_xy, n_xy, n_xy, n_gz, n_gz)],
        compiler_params=pltpu.CompilerParams(collective_id=0, has_side_effects=True),
    )(sums)
    wide = jax.ShapeDtypeStruct((channels, 27 * channels), F32)
    back_step, refine_step, mix_step = pl.pallas_call(
        finish_kernel,
        out_shape=(wide, wide, jax.ShapeDtypeStruct((channels, channels), F32)),
        in_specs=[VMEM],
        out_specs=(VMEM,) * 3,
    )(totals)
    return (vgrad.reshape(depth, rows, width), back_step, refine_step, mix_step)


def solution(mesh):
    in_specs = (
        P("gz", "xy", None),
        P(),
        P(),
        P(),
        P("gz", "xy", None, None, None, None, None),
        P("gz", "xy", None, None),
        P("gz", None, None),
    )
    out_specs = (P("gz", "xy", None), P(), P(), P())
    return jax.shard_map(body, mesh=mesh, in_specs=in_specs, out_specs=out_specs, check_vma=False)
```

profile of v0, /device:TPU:0, one launch (start us, length us, event | category | flops | bytes accessed | tf_op | source)
XLA Modules:
  0.0 64.6 jit_solution(15769973267139156681)
XLA Ops:
  0.6 0.0 copy-start
  0.6 1.8 %copy.21 = bf16[8,8,16,128]{3,2,1,0:T(8,128)(2,1)} copy(bf16[8,8,16,128]{3,1,2,0:T(8,128)(2,1)} %bitcast.29) | data formatting | bytes 524288
  2.4 8.4 %shard_map.102.vol = bf16[10,10,16,128]{3,2,1,0:T(8,128)(2,1)} custom-call(bf16[8,8,16,128]{3,2,1,0:T(8,128)(2,1)} %copy.21), custom_call_target="tpu_custom_call" | custom-call | tf_op jit(solution)/shard_map/pallas_call | solution.py:81
  10.9 0.0 copy-done
  10.9 0.5 reshape.44
  11.4 0.0 copy-start.3
  11.4 0.8 %dot_general.8 = bf16[8,8,4,128,16]{3,2,1,0,4:T(4,128)(2,1)S(1)} reshape(bf16[32768,16]{0,1:T(8,128)(2,1)S(1)} %bitcast.27) | data formatting | bytes 2097152 | tf_op jit(solution)/shard_map/dot_general | solution.py:401
  12.2 0.0 copy-done.3
  12.2 0.1 copy.13
  12.3 0.1 eq.25
  12.4 0.0 copy-start.2
  12.4 0.7 %copy-done.2 = s32[1,8,8]{2,1,0:T(8,128)S(1)} copy-done((s32[1,8,8]{2,1,0:T(8,128)S(1)}, s32[1,8,8]{2,1,0:T(8,128)}, u32[]{:S(2)}) %copy-start.2) | copy-done | bytes 280
  13.1 0.1 fusion.1
  13.2 0.1 iota_compare_fusion
  13.2 0.1 lt.23
  13.3 0.7 %convolution_bitcast_fusion = f32[8,8,4,4,128]{4,2,3,1,0:T(4,128)S(1)} fusion(bf16[8,8,4,128,16]{3,2,1,0,4:T(4,128)(2,1)S(1)} %dot_general.8, s32[16]{0:T(128)S(1)} %eq.25, pred[16]{0:T(512)(128)(4,1)S(1)} %lt.23), kind=kOutput, calls=%fused_computation | convolution fusion | flops 4194432 | bytes 1572944 | tf_op jit(solution)/shard_map/dot_general | solution.py:401
  14.0 0.9 %copy.15 = f32[8,8,4,4,128]{4,3,2,1,0:T(4,128)} copy(f32[8,8,4,4,128]{4,2,3,1,0:T(4,128)S(1)} %convolution_bitcast_fusion) | data formatting | bytes 1048576 | tf_op jit(solution)/shard_map/transpose | solution.py:404
  14.9 7.0 %shard_map.103 = (bf16[8,8,16,128]{3,2,1,0:T(8,128)(2,1)}, bf16[896,128]{1,0:T(8,128)(2,1)}, bf16[64,128]{1,0:T(8,128)(2,1)}) custom-call(bf16[10,10,16,128]{3,2,1,0:T(8,128)(2,1)} %shard_map.102.vol, f32[8,8,16,128]{3,2,1,0:T(8,128)} %bitcast.28, bf16[64,1728]{1,0:T(8,128)(2,1)} %back.3, bf16[64,1728]{1,0:T(8,128)(2,1)} %refine.1, bf16[64,64]{1,0:T(8,128)(2,1)} %mix.1), custom_call_target="tpu_custom_call" | custom-call | tf_op jit(solution)/shard_map/pallas_call | solution.py:409
  21.9 8.0 %shard_map.104.grad = bf16[10,10,16,128]{3,2,1,0:T(8,128)(2,1)} custom-call(bf16[8,8,16,128]{3,2,1,0:T(8,128)(2,1)} %get-tuple-element.12.block), custom_call_target="tpu_custom_call" | custom-call | tf_op jit(solution)/shard_map/pallas_call | solution.py:81
  29.9 4.5 %shard_map.105 = (bf16[8,8,16,128]{3,2,1,0:T(8,128)(2,1)}, bf16[2048,128]{1,0:T(8,128)(2,1)}) custom-call(bf16[10,10,16,128]{3,2,1,0:T(8,128)(2,1)} %shard_map.102.vol, bf16[10,10,16,128]{3,2,1,0:T(8,128)(2,1)} %shard_map.104.grad, bf16[64,1728]{1,0:T(8,128)(2,1)} %back.3, bf16[896,128]{1,0:T(8,128)(2,1)} %get-tuple-element.13.rsum, ...), custom_call_target="tpu_custom_call" | custom-call | tf_op jit(solution)/shard_map/pallas_call | solution.py:439
  34.4 26.7 %shard_map.106.totals = bf16[2048,128]{1,0:T(8,128)(2,1)} custom-call(bf16[2048,128]{1,0:T(8,128)(2,1)} %get-tuple-element.16.sums), custom_call_target="tpu_custom_call" | custom-call | tf_op jit(solution)/shard_map/pallas_call | solution.py:454
  61.1 0.0 copy-start.1
  61.1 2.7 %shard_map.107 = (f32[64,1728]{1,0:T(8,128)}, f32[64,1728]{1,0:T(8,128)}, f32[64,64]{1,0:T(8,128)}) custom-call(bf16[2048,128]{1,0:T(8,128)(2,1)} %shard_map.106.totals), custom_call_target="tpu_custom_call" | custom-call | tf_op jit(solution)/shard_map/pallas_call | solution.py:469
  63.8 0.0 copy-done.1
  63.8 0.8 %reshape.46 = bf16[8,8,2048]{2,1,0:T(8,128)(2,1)} reshape(bf16[8,8,16,128]{3,2,1,0:T(8,128)(2,1)S(1)} %copy-done.1) | data formatting | bytes 524288 | tf_op jit(solution)/shard_map/reshape | solution.py:475
  (1 shorter events, 0.0 us)
Async XLA Ops:
  0.6 10.2 %copy-start = (bf16[1,1,8,2,8,8,512]{6,5,4,3,2,1,0:T(8,128)(2,1)S(1)}, bf16[1,1,8,2,8,8,512]{6,5,4,3,2,1,0:T(8,128)(2,1)}, u32[]{:S(2)}) copy-start(bf16[1,1,8,2,8,8,512]{6,5,4,3,2,1,0:T(8,128)(2,1)} %param.11) | copy-start | bytes 3145732
  11.4 0.8 %copy-start.3 = (s32[1,1,8,2]{2,3,1,0:T(2,128)S(1)}, s32[1,1,8,2]{2,3,1,0:T(2,128)}, u32[]{:S(2)}) copy-start(s32[1,1,8,2]{2,3,1,0:T(2,128)} %param.12) | copy-start | bytes 196
  12.4 0.7 %copy-start.2 = (s32[1,8,8]{2,1,0:T(8,128)S(1)}, s32[1,8,8]{2,1,0:T(8,128)}, u32[]{:S(2)}) copy-start(s32[1,8,8]{2,1,0:T(8,128)} %param.13) | copy-start | bytes 772
  61.1 2.7 %copy-start.1 = (bf16[8,8,16,128]{3,2,1,0:T(8,128)(2,1)S(1)}, bf16[8,8,16,128]{3,2,1,0:T(8,128)(2,1)}, u32[]{:S(2)}) copy-start(bf16[8,8,16,128]{3,2,1,0:T(8,128)(2,1)} %get-tuple-element.15) | copy-start | bytes 786436
where the time goes:
time: 65.4 us; the launch traced here: 64.6 us
  Pallas kernels  57.3 us (88%)
  local copies, waits for them, and re-layouts  5.8 us (9%)
  between operations  0.72 us (1%)
  matrix products  0.68 us (1%)
    pallas_call x1, Pallas kernels, body(): pl.pallas_call(functools.partial(total_kernel, n_gz, n_xy), out_shape=jax...  26.7 us
    pallas_call x2, Pallas kernels, with_rims(): pl.pallas_call(functools.partial(rim_kernel, n_gz, n_xy), out_shape=jax.S...  16.4 us
    pallas_call x1, Pallas kernels, body(): pl.pallas_call(functools.partial(refine_kernel, period), out_shape=(jax.S...  7 us
    pallas_call x1, Pallas kernels, body(): pl.pallas_call(backbone_kernel, out_shape=(jax.ShapeDtypeStruct(brick, BF...  4.48 us
    pallas_call x1, Pallas kernels, body(): pl.pallas_call(finish_kernel, out_shape=(wide, wide, jax.ShapeDtypeStruct...  2.68 us
    unnamed x10, local copies, waits for them, and re-layouts  2.57 us

commit v1 on v0

v1 whole, which is shorter than its diff:
```python
import functools

import jax
import jax.numpy as jnp
from jax import lax
from jax.experimental import pallas as pl
from jax.experimental.pallas import tpu as pltpu
from jax.sharding import PartitionSpec as P

EPSILON = 1e-06
F32 = jnp.float32
BF16 = jnp.bfloat16
VMEM = pl.BlockSpec(memory_space=pltpu.VMEM)
ANY = pl.BlockSpec(memory_space=pl.ANY)
MESH = pl.DeviceIdType.MESH


def neighbours():
    return [(dz, dy) for dz in (-1, 0, 1) for dy in (-1, 0, 1) if (dz, dy) != (0, 0)]


def near(step, size):
    if step == 0:
        return pl.ds(1, size)
    return pl.ds(size, 1) if step > 0 else pl.ds(1, 1)


def far(step, size):
    if step == 0:
        return pl.ds(1, size)
    return pl.ds(0, 1) if step > 0 else pl.ds(size + 1, 1)


class Rims:
    def __init__(self, sizes, place, framed, depth, rows, lanes, send, recv):
        self.sizes, self.place, self.framed = sizes, place, framed
        self.depth, self.rows, self.lanes = depth, rows, lanes
        self.send, self.recv = send, recv

    def there(self, dz, dy):
        (n_gz, n_xy), (gz, xy) = self.sizes, self.place
        inside = (gz + dz >= 0) & (gz + dz < n_gz) & (xy + dy >= 0) & (xy + dy < n_xy)
        return inside, (gz + dz, xy + dy)

    def copy(self, dz, dy, number):
        cells = (slice(None), pl.ds(0, self.lanes))
        return pltpu.make_async_remote_copy(
            src_ref=self.framed.at[(near(dz, self.depth), near(dy, self.rows)) + cells],
            dst_ref=self.framed.at[(far(dz, self.depth), far(dy, self.rows)) + cells],
            send_sem=self.send.at[number],
            recv_sem=self.recv.at[number],
            device_id=self.there(dz, dy)[1],
            device_id_type=MESH,
        )

    def start(self):
        for number, (dz, dy) in enumerate(neighbours()):

            @pl.when(self.there(dz, dy)[0])
            def _():
                self.copy(dz, dy, number).start()

    def wait_recv(self):
        for number, (dz, dy) in enumerate(neighbours()):

            @pl.when(self.there(-dz, -dy)[0])
            def _():
                self.copy(dz, dy, number).wait_recv()

    def wait_send(self):
        for number, (dz, dy) in enumerate(neighbours()):

            @pl.when(self.there(dz, dy)[0])
            def _():
                self.copy(dz, dy, number).wait_send()


class Plane:
    def __init__(self, n_gz, n_xy, n_x):
        gz, xy = lax.axis_index("gz"), lax.axis_index("xy")
        self.n_x = n_x
        self.members, self.levels = n_gz * n_x, n_xy // n_x
        self.level, self.x = lax.div(xy, n_x), lax.rem(xy, n_x)
        self.me = gz * n_x + self.x
        self.gz = gz

    def member(self, step):
        who = lax.rem(self.me + step, self.members)
        return who, (lax.div(who, self.n_x), self.level * self.n_x + lax.rem(who, self.n_x))

    def above(self, step):
        level = lax.rem(self.level + step, self.levels)
        return self.gz, level * self.n_x + self.x


def each(count, action):
    def one(step, carry):
        action(step)
        return carry

    lax.fori_loop(1, count, one, 0)


class Total:
    def __init__(self, plane, sums, got, level_got, out, sems):
        self.plane, self.sums, self.got, self.level_got, self.out = plane, sums, got, level_got, out
        self.sems = sems
        self.chunk = got.shape[1]
        self.own = pl.ds(pl.multiple_of(plane.me * self.chunk, self.chunk), self.chunk)

    def remote(self, stage, step, source, target, device):
        return pltpu.make_async_remote_copy(
            src_ref=source,
            dst_ref=target,
            send_sem=self.sems[2 * stage].at[step],
            recv_sem=self.sems[2 * stage + 1].at[step],
            device_id=device,
            device_id_type=MESH,
        )

    def scatter(self, step):
        who, device = self.plane.member(step)
        part = pl.ds(pl.multiple_of(who * self.chunk, self.chunk), self.chunk)
        return self.remote(0, step, self.sums.at[part], self.got.at[step], device)

    def column(self, step):
        here = self.level_got.at[self.plane.level]
        return self.remote(1, step, here, here, self.plane.above(step))

    def gather(self, step):
        here = self.out.at[self.own]
        return self.remote(2, step, here, here, self.plane.member(step)[1])

    def start(self):
        each(self.plane.members, lambda step: self.scatter(step).start())

    def middle(self):
        each(self.plane.members, lambda step: self.scatter(step).wait_recv())
        total = self.sums[self.own, :].astype(F32)
        for step in range(1, self.plane.members):
            total = total + self.got[step].astype(F32)
        self.level_got[self.plane.level] = total.astype(BF16)
        each(self.plane.levels, lambda step: self.column(step).start())

    def spread(self):
        each(self.plane.levels, lambda step: self.column(step).wait_recv())
        total = self.level_got[0].astype(F32)
        for level in range(1, self.plane.levels):
            total = total + self.level_got[level].astype(F32)
        self.out[self.own, :] = total.astype(BF16)
        each(self.plane.members, lambda step: self.gather(step).start())

    def finish(self):
        each(self.plane.members, lambda step: self.gather(step).wait_recv())

    def drain(self):
        each(self.plane.members, lambda step: self.scatter(step).wait_send())
        each(self.plane.levels, lambda step: self.column(step).wait_send())
        each(self.plane.members, lambda step: self.gather(step).wait_send())


def weight_halves(weight, half, turned):
    lows, highs = [], []
    count = weight.shape[1] // half
    for first in range(0, count, 2):
        if first + 1 < count:
            near = weight[:, pl.ds(first * half, 2 * half)].astype(F32)
        else:
            last = weight[:, pl.ds(first * half, half)].astype(F32)
            near = jnp.concatenate([last, jnp.zeros_like(last)], axis=1)
        far = pltpu.roll(near, half, 1)
        if turned:
            both = jnp.concatenate([near, far], axis=0).T
            near, far = both[:half], both[half:]
        lows += [near, far]
        highs += [far, near]
    return lows, highs


def fill_band(target, weight, turned):
    half = weight.shape[0]
    lows, highs = weight_halves(weight, half, turned)
    low = lax.broadcasted_iota(jnp.int32, (half, 2 * half), 1) < half
    for offset in range(9):
        ks = [26 - 3 * offset - x if turned else 3 * offset + x for x in range(3)]
        parts = [
            jnp.where(low, lows[ks[1]], highs[ks[0]]),
            jnp.where(low, lows[ks[2]], highs[ks[1]]),
            jnp.where(low, 0.0, highs[ks[2]]),
            jnp.where(low, lows[ks[0]], 0.0),
        ]
        for place, part in enumerate(parts):
            target[pl.ds((4 * offset + place) * half, half), :] = part.astype(BF16)


def side_lanes(cells, half, period):
    pairs = cells.shape[1]
    lane = lax.broadcasted_iota(jnp.int32, cells.shape, 2)
    place = lax.broadcasted_iota(jnp.int32, cells.shape, 1) % period
    right = pltpu.roll(cells, pairs - 1, 1)
    left = pltpu.roll(cells, 1, 1)
    low = lane < half
    right = jnp.where(place == period - 1, 0.0, right)
    left = jnp.where(place == 0, 0.0, left)
    return jnp.where(low, right, left)


def fill_windows(target, source, half, period, inner):
    depth = target.shape[0]
    lanes = 2 * half
    if inner:
        target[...] = jnp.zeros_like(target)
    first, last = (1, depth - 1) if inner else (0, depth)
    for z in range(first, last):
        cells = source(z - first)
        rows = pl.ds(1, target.shape[1] - 2) if inner else pl.ds(0, target.shape[1])
        target[z, rows, :, pl.ds(0, lanes)] = cells.astype(BF16)
        target[z, rows, :, pl.ds(lanes, lanes)] = side_lanes(cells.astype(F32), half, period).astype(
            BF16
        )


def window_rows(windows, z, count, dz, dy):
    rows = windows.shape[1] - 2
    pairs, width = windows.shape[2], windows.shape[3]
    part = windows[pl.ds(z + dz, count), pl.ds(dy, rows)]
    return part.reshape(count * rows * pairs, width)


def conv_rows(windows, weight, z, count):
    parts = [window_rows(windows, z, count, dz, dy) for dz in range(3) for dy in range(3)]
    return jnp.dot(jnp.concatenate(parts, axis=1), weight[...], preferred_element_type=F32)


def outer_sums(out, base, windows, grad_turned, half):
    depth = windows.shape[0] - 2
    lanes = 2 * half
    lane = lax.broadcasted_iota(jnp.int32, (half, lanes), 1)
    held = None
    for offset in range(9):
        both = jnp.dot(
            grad_turned,
            window_rows(windows, 0, depth, offset // 3, offset % 3),
            preferred_element_type=F32,
        )
        top_near, top_far = both[:half, :lanes], both[:half, lanes:]
        far_turned = pltpu.roll(top_far, half, 1)
        near_turned = pltpu.roll(top_near, half, 1)
        first = jnp.where(lane < half, far_turned, near_turned) + both[half:, :lanes]
        third = near_turned + both[half:, lanes:]
        out[pl.ds(base + offset * half, half), :] = first.astype(BF16)
        if offset % 2 == 0:
            held = jnp.where(lane < half, third, 0.0)
        else:
            pair = held + jnp.where(lane < half, 0.0, pltpu.roll(third, half, 1))
            out[pl.ds(base + (9 + offset // 2) * half, half), :] = pair.astype(BF16)
    out[pl.ds(base + 13 * half, half), :] = held.astype(BF16)


def clear_frame(framed):
    depth, rows = framed.shape[0], framed.shape[1]
    for z in (0, depth - 1):
        framed[z] = jnp.zeros(framed.shape[1:], framed.dtype)
    side = (depth - 2, 1) + framed.shape[2:]
    for y in (0, rows - 1):
        framed[pl.ds(1, depth - 2), pl.ds(y, 1)] = jnp.zeros(side, framed.dtype)


def frame_sides(framed, half):
    depth, rows = framed.shape[0], framed.shape[1]
    pairs, lanes = framed.shape[2], 2 * half

    def fill(zs, ys):
        cells = framed[zs, ys, :, pl.ds(0, lanes)].reshape(-1, pairs, lanes).astype(F32)
        turned = side_lanes(cells, half, pairs).astype(BF16)
        framed[zs, ys, :, pl.ds(lanes, lanes)] = turned.reshape(zs.size, ys.size, pairs, lanes)

    for z in (0, depth - 1):
        fill(pl.ds(z, 1), pl.ds(0, rows))
    for y in (0, rows - 1):
        fill(pl.ds(1, depth - 2), pl.ds(y, 1))


def step_kernel(
    n_gz, n_xy, n_x, period,
    vol_h, cot_h, back_h, refine_h, mix_h, slot_h, count_h,
    vgrad_h, tot_a, tot_b,
    vin, cin, back, refine, mix, slot, count, vout,
    tall, cot, xw, fw, pw, gw, wb, wr, wrt, wbt, gate_s, pg_s,
    sum_a, sum_b, got_a, got_b, level_a, level_b,
    local, rim_send, rim_recv, grad_send, grad_recv, *sems,
):
    depth, pairs, rows, lanes = vin.shape
    half = lanes // 2
    slots, tiles = cin.shape[0], pairs // period
    capacity = slot.shape[0]
    step = 4 if depth % 4 == 0 else depth
    flat = step * rows * pairs
    block = 14 * half
    gz, xy = lax.axis_index("gz"), lax.axis_index("xy")
    place, sizes = (gz, xy), (n_gz, n_xy)
    plane = Plane(n_gz, n_xy, n_x)
    rims = Rims(sizes, place, xw, depth, rows, lanes, rim_send, rim_recv)
    grad_rims = Rims(sizes, place, gw, depth, rows, lanes, grad_send, grad_recv)
    total_a = Total(plane, sum_a, got_a, level_a, tot_a, sems[:6])
    total_b = Total(plane, sum_b, got_b, level_b, tot_b, sems[6:])

    loads = [
        pltpu.make_async_copy(source, target, local.at[number])
        for number, (source, target) in enumerate(
            (
                (vol_h, vin), (back_h, back), (refine_h, refine), (mix_h, mix),
                (slot_h, slot), (count_h, count), (cot_h, cin),
            )
        )
    ]
    for load in loads:
        load.start()
    for framed in (xw, gw, fw, pw):
        clear_frame(framed)

    barrier = pltpu.get_barrier_semaphore()

    def greet(device):
        pl.semaphore_signal(barrier, inc=1, device_id=device, device_id_type=MESH)

    for dz, dy in neighbours():
        inside, where = rims.there(dz, dy)

        @pl.when(inside)
        def _():
            greet(where)

    each(plane.members, lambda step: greet(plane.member(step)[1]))
    each(plane.levels, lambda step: greet(plane.above(step)))

    loads[0].wait()

    def turn_in(z, carry):
        tall[pl.ds(pl.multiple_of(z * pairs * rows, 8), pairs * rows), :] = (
            vin[z].astype(F32).reshape(pairs * rows, lanes)
        )
        for y in range(rows):
            cells = tall[pl.ds(z * pairs * rows + y, pairs, stride=rows), :]
            xw[z + 1, y + 1, :, pl.ds(0, lanes)] = cells.astype(BF16)
        return carry

    lax.fori_loop(0, depth, turn_in, 0)

    across = 1 + lax.min(gz, 1) + lax.min(n_gz - 1 - gz, 1)
    along = 1 + lax.min(xy, 1) + lax.min(n_xy - 1 - xy, 1)
    pl.semaphore_wait(barrier, across * along - 1 + plane.members - 1 + plane.levels - 1)
    rims.start()

    inner = pl.ds(1, rows)

    def own_sides(z, carry):
        cells = xw[z + 1, inner, :, pl.ds(0, lanes)].astype(F32)
        xw[z + 1, inner, :, pl.ds(lanes, lanes)] = side_lanes(cells, half, pairs).astype(BF16)
        return carry

    lax.fori_loop(0, depth, own_sides, 0)
    loads[1].wait()
    fill_band(wb, back, False)
    loads[2].wait()
    fill_band(wr, refine, False)
    fill_band(wrt, refine, True)
    fill_band(wbt, back, True)
    loads[3].wait()
    mixed = mix[...].astype(F32)
    mixed = jnp.concatenate([mixed, jnp.zeros_like(mixed)], axis=1)
    mix2 = jnp.concatenate([mixed, pltpu.roll(mixed, half, 1)], axis=0).T.astype(BF16)

    for load in loads[4:]:
        load.wait()
    picks = []
    for number in range(slots):
        owner, place_in = number // capacity, number % capacity
        live = place_in < count[xy, owner]
        which = slot[place_in, owner]
        picks.append([jnp.where(live & (which == tile), 1.0, 0.0) for tile in range(tiles)])

    def pick(z, carry):
        held = [None] * tiles
        for number in range(slots):
            cells = cin[number, z].astype(F32)
            for tile in range(tiles):
                term = cells * picks[number][tile]
                held[tile] = term if held[tile] is None else held[tile] + term
        span = period * rows
        for tile in range(tiles):
            start = pl.multiple_of(z * pairs * rows + tile * span, 8)
            tall[pl.ds(start, span), :] = held[tile].reshape(span, lanes)
        for y in range(rows):
            cot[z, y] = tall[pl.ds(z * pairs * rows + y, pairs, stride=rows), :]
        return carry

    lax.fori_loop(0, depth, pick, 0)

    rims.wait_recv()
    frame_sides(xw, half)

    def put(target, z, cells, period):
        target[pl.ds(z + 1, step), inner, :, pl.ds(0, lanes)] = cells.astype(BF16)
        close = cells.astype(F32).reshape(step * rows, pairs, lanes)
        target[pl.ds(z + 1, step), inner, :, pl.ds(lanes, lanes)] = (
            side_lanes(close, half, period).astype(BF16).reshape(step, rows, pairs, lanes)
        )

    brick = (step, rows, pairs, lanes)
    for z in range(0, depth, step):
        own = xw[pl.ds(z + 1, step), inner, :, pl.ds(0, lanes)].astype(F32).reshape(flat, lanes)
        feature = (own + conv_rows(xw, wb, z, step)).astype(BF16)
        put(fw, z, feature.reshape(brick), period)
    for z in range(0, depth, step):
        pre = conv_rows(fw, wr, z, step)
        sig = jax.nn.sigmoid(pre)
        upstream = cot[pl.ds(z, step)].reshape(flat, lanes).astype(BF16)
        gate_s[pl.ds(z * rows * pairs, flat), :] = (pre * sig).astype(BF16)
        gated_grad = jnp.dot(upstream, mix2, preferred_element_type=F32)
        pre_grad = (gated_grad * sig * (1.0 + pre * (1.0 - sig))).astype(BF16)
        pg_s[pl.ds(z * rows * pairs, flat), :] = pre_grad
        put(pw, z, pre_grad.reshape(brick), period)

    outer_sums(sum_a, 0, fw, pg_s[...].T, half)
    cot_rows = cot[...].reshape(depth * rows * pairs, lanes).astype(BF16)
    both = jnp.dot(gate_s[...].T, cot_rows, preferred_element_type=F32)
    lane = lax.broadcasted_iota(jnp.int32, (half, lanes), 1)
    sum_a[pl.ds(block, half), :] = jnp.where(
        lane < half, both[:half] + pltpu.roll(both[half:], half, 1), 0.0
    ).astype(BF16)
    used = block + half
    if used < sum_a.shape[0]:
        sum_a[pl.ds(used, sum_a.shape[0] - used), :] = jnp.zeros((sum_a.shape[0] - used, lanes), BF16)
    total_a.start()

    for z in range(0, depth, step):
        upstream = cot[pl.ds(z, step)].reshape(flat, lanes)
        grad = (upstream + conv_rows(pw, wrt, z, step)).astype(BF16)
        put(gw, z, grad.reshape(brick), pairs)
    grad_rims.start()

    own = gw[pl.ds(1, depth), inner, :, pl.ds(0, lanes)].reshape(depth * rows * pairs, lanes)
    outer_sums(sum_b, 0, xw, own.T, half)
    if block < sum_b.shape[0]:
        sum_b[pl.ds(block, sum_b.shape[0] - block), :] = jnp.zeros((sum_b.shape[0] - block, lanes), BF16)
    total_b.start()
    total_a.middle()

    grad_rims.wait_recv()
    frame_sides(gw, half)

    def back_conv(z):
        own = gw[pl.ds(z + 1, step), inner, :, pl.ds(0, lanes)].astype(F32).reshape(flat, lanes)
        tall[pl.ds(z * rows * pairs, flat), :] = own + conv_rows(gw, wbt, z, step)

    back_conv(0)
    total_b.middle()
    for z in range(step, depth, step):
        back_conv(z)
    total_a.spread()

    def turn_out(z, carry):
        for pair in range(pairs):
            cells = tall[pl.ds(z * pairs * rows + pair, rows, stride=pairs), :]
            vout[z, pair] = cells.astype(BF16)
        return carry

    lax.fori_loop(0, depth, turn_out, 0)
    store = pltpu.make_async_copy(vout, vgrad_h, local.at[len(loads)])
    store.start()
    total_b.spread()
    total_a.finish()
    total_b.finish()
    rims.wait_send()
    grad_rims.wait_send()
    total_a.drain()
    total_b.drain()
    store.wait()


def finish_kernel(tot_a, tot_b, back_step, refine_step, mix_step):
    half = mix_step.shape[0]
    lanes = 2 * half
    block = 14 * half
    low = lax.broadcasted_iota(jnp.int32, (half, lanes), 1) < half

    def scale_of(values, count):
        squares = jnp.sum(values * values, axis=0, keepdims=True)
        return jnp.sqrt(jnp.sum(squares, axis=1, keepdims=True) / count + EPSILON)

    for totals, out in ((tot_b, back_step), (tot_a, refine_step)):
        values = totals[pl.ds(0, block), :].astype(F32)
        scale = scale_of(values, 27.0 * half * half)
        lows, highs = [None] * 28, [None] * 28
        for tile in range(14):
            near = values[tile * half : (tile + 1) * half]
            both = jnp.concatenate([near, pltpu.roll(near, half, 1)], axis=0).T / scale
            if tile < 9:
                first, second = 3 * tile, 3 * tile + 1
            else:
                first, second = 6 * (tile - 9) + 2, 6 * (tile - 9) + 5
            lows[first], highs[first] = both[:half], both[half:]
            if second < 27:
                lows[second], highs[second] = both[half:], both[:half]
        for k in range(0, 26, 2):
            out[:, pl.ds(k * half, lanes)] = jnp.where(low, lows[k], highs[k + 1])
        out[:, pl.ds(26 * half, half)] = lows[26][:, :half]
    values = tot_a[pl.ds(block, half), :].astype(F32)
    mix_step[...] = (values / scale_of(values, 1.0 * half * half))[:, :half]


def body(volume, backbone_weight, refine_weight, mix_weight, tile_cot, tile_slot, tile_count):
    depth, rows, width = volume.shape
    channels = mix_weight.shape[0]
    edge = tile_cot.shape[4]
    owners, capacity = tile_cot.shape[2], tile_cot.shape[3]
    assert depth == edge and rows == edge
    lanes = 2 * channels
    pairs = width // lanes
    period = edge // 2
    slots = owners * capacity
    n_gz, n_xy = lax.axis_size("gz"), lax.axis_size("xy")
    n_x = max(n_gz // 2, 1)
    if n_xy % n_x:
        n_x = 1
    members, levels = n_gz * n_x, n_xy // n_x

    vol = volume.reshape(depth, rows, pairs, lanes).transpose(0, 2, 1, 3)
    cot = tile_cot.reshape(slots, edge, edge, period, lanes).transpose(0, 1, 3, 2, 4)
    slot = tile_slot.reshape(owners, capacity).T
    count = tile_count.reshape(owners, owners)

    block = 14 * channels
    chunk_a = -(-(block + channels) // (members * 16)) * 16
    chunk_b = -(-block // (members * 16)) * 16
    framed = pltpu.VMEM((depth + 2, rows + 2, pairs, 2 * lanes), BF16)
    band = pltpu.VMEM((36 * channels, lanes), BF16)
    cells = depth * rows * pairs
    dma = pltpu.SemaphoreType.DMA
    vgrad, tot_a, tot_b = pl.pallas_call(
        functools.partial(step_kernel, n_gz, n_xy, n_x, period),
        out_shape=(
            jax.ShapeDtypeStruct(vol.shape, BF16),
            jax.ShapeDtypeStruct((members * chunk_a, lanes), BF16),
            jax.ShapeDtypeStruct((members * chunk_b, lanes), BF16),
        ),
        in_specs=[ANY] * 7,
        out_specs=(ANY, VMEM, VMEM),
        scratch_shapes=[
            pltpu.VMEM(vol.shape, BF16),
            pltpu.VMEM(cot.shape, BF16),
            pltpu.VMEM(backbone_weight.shape, BF16),
            pltpu.VMEM(refine_weight.shape, BF16),
            pltpu.VMEM(mix_weight.shape, BF16),
            pltpu.SMEM(slot.shape, jnp.int32),
            pltpu.SMEM(count.shape, jnp.int32),
            pltpu.VMEM(vol.shape, BF16),
            pltpu.VMEM((cells, lanes), F32),
            pltpu.VMEM((depth, rows, pairs, lanes), F32),
            framed, framed, framed, framed,
            band, band, band, band,
            pltpu.VMEM((cells, lanes), BF16),
            pltpu.VMEM((cells, lanes), BF16),
            pltpu.VMEM((members * chunk_a, lanes), BF16),
            pltpu.VMEM((members * chunk_b, lanes), BF16),
            pltpu.VMEM((members, chunk_a, lanes), BF16),
            pltpu.VMEM((members, chunk_b, lanes), BF16),
            pltpu.VMEM((levels, chunk_a, lanes), BF16),
            pltpu.VMEM((levels, chunk_b, lanes), BF16),
            dma((8,)),
            dma((8,)), dma((8,)), dma((8,)), dma((8,)),
        ]
        + [dma((n,)) for n in (members, members, levels, levels, members, members)] * 2,
        compiler_params=pltpu.CompilerParams(
            collective_id=0, has_side_effects=True, vmem_limit_bytes=56 * 1024 * 1024
        ),
    )(vol, cot, backbone_weight, refine_weight, mix_weight, slot, count)
    wide = jax.ShapeDtypeStruct((channels, 27 * channels), F32)
    back_step, refine_step, mix_step = pl.pallas_call(
        finish_kernel,
        out_shape=(wide, wide, jax.ShapeDtypeStruct((channels, channels), F32)),
        in_specs=[VMEM] * 2,
        out_specs=(VMEM,) * 3,
    )(tot_a, tot_b)
    vgrad = vgrad.transpose(0, 2, 1, 3).reshape(depth, rows, width)
    return (vgrad, back_step, refine_step, mix_step)


def solution(mesh):
    in_specs = (
        P("gz", "xy", None),
        P(),
        P(),
        P(),
        P("gz", "xy", None, None, None, None, None),
        P("gz", "xy", None, None),
        P("gz", None, None),
    )
    out_specs = (P("gz", "xy", None), P(), P(), P())
    return jax.shard_map(body, mesh=mesh, in_specs=in_specs, out_specs=out_specs, check_vma=False)
```

time: 65.4 us -> 37.4 us (0.57)
  Pallas kernels: 57.3 us -> 35.8 us
  local copies, waits for them, and re-layouts: 5.8 us -> 0.71 us
  matrix products: 0.68 us -> 0 us
    pallas_call x5 -> x1, Pallas kernels: 54.6 us -> 33.2 us  [body(): pl.pallas_call(functools.partial(step_kernel, n_gz, n_xy, n_x, period), o...]
    unnamed x10 -> x3, local copies, waits for them, and re-layouts: 2.57 us -> 0.71 us
    reshape x2 -> x0, local copies, waits for them, and re-layouts: 1.35 us -> none  [the longest x1 0.82 us: body(): return (vgrad.reshape(depth, rows, width), back_step, refine_step, mix_step)]
    transpose x1 -> x0, local copies, waits for them, and re-layouts: 0.94 us -> none  [body(): cot.reshape(tiles, depth, rows, period, lanes).transpose(1, 2, 0, 3, 4)]
    dot_general x1 -> x0, local copies, waits for them, and re-layouts: 0.78 us -> none  [body(): jnp.dot(picker, tile_cot.reshape(slots, edge * edge * edge * channels), p...]
    dot_general x1 -> x0, matrix products: 0.68 us -> none  [body(): jnp.dot(picker, tile_cot.reshape(slots, edge * edge * edge * channels), p...]
where the time goes in v1:
time: 37.4 us; the launch traced here: 37.2 us
  Pallas kernels  35.8 us (96%)
  local copies, waits for them, and re-layouts  0.71 us (2%)
  between operations  0.65 us (2%)
    pallas_call x1, Pallas kernels, body(): pl.pallas_call(functools.partial(step_kernel, n_gz, n_xy, n_x, period), o...  33.2 us
    pallas_call x1, Pallas kernels, body(): pl.pallas_call(finish_kernel, out_shape=(wide, wide, jax.ShapeDtypeStruct...  2.65 us

profile of v1, /device:TPU:0, one launch (start us, length us, event | category | flops | bytes accessed | tf_op | source)
XLA Modules:
  0.0 37.2 jit_solution(3267093426868504525)
XLA Ops:
  0.6 33.2 %shard_map.102 = (bf16[8,16,8,128]{3,2,1,0:T(8,128)(2,1)}, bf16[1024,128]{1,0:T(8,128)(2,1)}, bf16[896,128]{1,0:T(8,128)(2,1)}) custom-call(bf16[8,16,8,128]{3,2,1,0:T(8,128)(2,1)} %bitcast.14, bf16[16,8,4,8,128]{4,3,2,1,0:T(8,128)(2,1)} %bitcast.13, bf16[64,1728]{1,0:T(8,128)(2,1)} %back_h.1, bf16[64,1728]{1,0:T(8,128)(2,1)} %refine_h.1, ...), custom_call_target="tpu_custom_call" | custom-call | tf_op jit(solution)/shard_map/pallas_call | solution.py:541
  33.8 0.0 copy-start
  33.8 2.7 %shard_map.103 = (f32[64,1728]{1,0:T(8,128)}, f32[64,1728]{1,0:T(8,128)}, f32[64,64]{1,0:T(8,128)}) custom-call(bf16[1024,128]{1,0:T(8,128)(2,1)} %get-tuple-element.11.tot_a, bf16[896,128]{1,0:T(8,128)(2,1)} %get-tuple-element.12.tot_b), custom_call_target="tpu_custom_call" | custom-call | tf_op jit(solution)/shard_map/pallas_call | solution.py:580
  36.5 0.0 copy-done
  36.5 0.7 %copy.12 = bf16[8,8,2048]{2,1,0:T(8,128)(2,1)} copy(bf16[8,8,2048]{2,1,0:T(8,128)(2,1)S(1)} %bitcast.15) | data formatting | bytes 524288
Async XLA Ops:
  33.8 2.7 %copy-start = (bf16[8,16,8,128]{3,2,1,0:T(8,128)(2,1)S(1)}, bf16[8,16,8,128]{3,2,1,0:T(8,128)(2,1)}, u32[]{:S(2)}) copy-start(bf16[8,16,8,128]{3,2,1,0:T(8,128)(2,1)} %get-tuple-element.10) | copy-start | bytes 786436

commit v2 on v1

--- a/solution.py
+++ b/solution.py
@@ -12,6 +12,7 @@
 BF16 = jnp.bfloat16
 VMEM = pl.BlockSpec(memory_space=pltpu.VMEM)
 ANY = pl.BlockSpec(memory_space=pl.ANY)
+HBM = pl.BlockSpec(memory_space=pltpu.HBM)
 MESH = pl.DeviceIdType.MESH
 
 
@@ -179,8 +180,9 @@
 
 def fill_band(target, weight, turned):
     half = weight.shape[0]
+    lanes = 2 * half
     lows, highs = weight_halves(weight, half, turned)
-    low = lax.broadcasted_iota(jnp.int32, (half, 2 * half), 1) < half
+    low = lax.broadcasted_iota(jnp.int32, (half, lanes), 1) < half
     for offset in range(9):
         ks = [26 - 3 * offset - x if turned else 3 * offset + x for x in range(3)]
         parts = [
@@ -189,8 +191,15 @@
             jnp.where(low, 0.0, highs[ks[2]]),
             jnp.where(low, lows[ks[0]], 0.0),
         ]
+        tile = 4 * (offset // 3) + offset % 3
         for place, part in enumerate(parts):
-            target[pl.ds((4 * offset + place) * half, half), :] = part.astype(BF16)
+            part = part.astype(BF16)
+            target[pl.ds((4 * tile + place) * half, half), pl.ds(0, lanes)] = part
+            target[pl.ds((4 * tile + 4 + place) * half, half), pl.ds(lanes, lanes)] = part
+    empty = jnp.zeros((4 * half, lanes), BF16)
+    for dz in range(3):
+        target[pl.ds((4 * dz + 3) * 4 * half, 4 * half), pl.ds(0, lanes)] = empty
+        target[pl.ds(4 * dz * 4 * half, 4 * half), pl.ds(lanes, lanes)] = empty
 
 
 def side_lanes(cells, half, period):
@@ -205,56 +214,50 @@
     return jnp.where(low, right, left)
 
 
-def fill_windows(target, source, half, period, inner):
-    depth = target.shape[0]
-    lanes = 2 * half
-    if inner:
-        target[...] = jnp.zeros_like(target)
-    first, last = (1, depth - 1) if inner else (0, depth)
-    for z in range(first, last):
-        cells = source(z - first)
-        rows = pl.ds(1, target.shape[1] - 2) if inner else pl.ds(0, target.shape[1])
-        target[z, rows, :, pl.ds(0, lanes)] = cells.astype(BF16)
-        target[z, rows, :, pl.ds(lanes, lanes)] = side_lanes(cells.astype(F32), half, period).astype(
-            BF16
-        )
-
-
 def window_rows(windows, z, count, dz, dy):
-    rows = windows.shape[1] - 2
     pairs, width = windows.shape[2], windows.shape[3]
-    part = windows[pl.ds(z + dz, count), pl.ds(dy, rows)]
-    return part.reshape(count * rows * pairs, width)
+    parts = [
+        windows[pl.ds(z + dz, count), y + dy].reshape(count * pairs, width)
+        for y in range(0, windows.shape[1] - 2, 2)
+    ]
+    return jnp.concatenate(parts, axis=0)
 
 
 def conv_rows(windows, weight, z, count):
-    parts = [window_rows(windows, z, count, dz, dy) for dz in range(3) for dy in range(3)]
+    parts = [window_rows(windows, z, count, dz, dy) for dz in range(3) for dy in range(4)]
     return jnp.dot(jnp.concatenate(parts, axis=1), weight[...], preferred_element_type=F32)
 
 
-def outer_sums(out, base, windows, grad_turned, half):
+def outer_sums(out, windows, grad_turned, half, step):
     depth = windows.shape[0] - 2
     lanes = 2 * half
-    lane = lax.broadcasted_iota(jnp.int32, (half, lanes), 1)
-    held = None
-    for offset in range(9):
-        both = jnp.dot(
-            grad_turned,
-            window_rows(windows, 0, depth, offset // 3, offset % 3),
-            preferred_element_type=F32,
-        )
-        top_near, top_far = both[:half, :lanes], both[:half, lanes:]
-        far_turned = pltpu.roll(top_far, half, 1)
-        near_turned = pltpu.roll(top_near, half, 1)
-        first = jnp.where(lane < half, far_turned, near_turned) + both[half:, :lanes]
-        third = near_turned + both[half:, lanes:]
-        out[pl.ds(base + offset * half, half), :] = first.astype(BF16)
-        if offset % 2 == 0:
-            held = jnp.where(lane < half, third, 0.0)
-        else:
-            pair = held + jnp.where(lane < half, 0.0, pltpu.roll(third, half, 1))
-            out[pl.ds(base + (9 + offset // 2) * half, half), :] = pair.astype(BF16)
-    out[pl.ds(base + 13 * half, half), :] = held.astype(BF16)
+    low = lax.broadcasted_iota(jnp.int32, (half, lanes), 1) < half
+    held = {}
+
+    def turn(values):
+        return pltpu.roll(values, half, 1)
+
+    for dz in range(3):
+        products = []
+        for dy in range(4):
+            seen = [window_rows(windows, z, step, dz, dy) for z in range(0, depth, step)]
+            seen = jnp.concatenate(seen, axis=0)
+            products.append(jnp.dot(grad_turned, seen, preferred_element_type=F32))
+        for dy in range(3):
+            both = products[dy][:lanes] + products[dy + 1][lanes:]
+            top_near, top_far = both[:half, :lanes], both[:half, lanes:]
+            last_near, last_far = both[half:, :lanes], both[half:, lanes:]
+            sums = ((top_far, last_near), (last_near, top_near), (top_near, last_far))
+            for dx, (right, left) in enumerate(sums):
+                k = 3 * (3 * dz + dy) + dx
+                tile = 2 * (k // 4) + k % 2
+                if k % 4 < 2:
+                    held[tile] = turn(right) + left
+                else:
+                    pair = jnp.where(low, held.pop(tile), right + turn(left))
+                    out[pl.ds(tile * half, half), :] = pair.astype(BF16)
+    for tile, values in held.items():
+        out[pl.ds(tile * half, half), :] = jnp.where(low, values, 0.0).astype(BF16)
 
 
 def clear_frame(framed):
@@ -284,10 +287,10 @@
 def step_kernel(
     n_gz, n_xy, n_x, period,
     vol_h, cot_h, back_h, refine_h, mix_h, slot_h, count_h,
-    vgrad_h, tot_a, tot_b,
-    vin, cin, back, refine, mix, slot, count, vout,
-    tall, cot, xw, fw, pw, gw, wb, wr, wrt, wbt, gate_s, pg_s,
-    sum_a, sum_b, got_a, got_b, level_a, level_b,
+    vgrad, tot_b, refine_step, mix_step,
+    vin, cin, back, refine, mix, slot, count,
+    tall, cot, xw, fw, pw, gw, wb, wr, wrt, wbt, gate_s, pg_s, own_s,
+    tot_a, sum_a, sum_b, got_a, got_b, level_a, level_b,
     local, rim_send, rim_recv, grad_send, grad_recv, *sems,
 ):
     depth, pairs, rows, lanes = vin.shape
@@ -295,7 +298,8 @@
     slots, tiles = cin.shape[0], pairs // period
     capacity = slot.shape[0]
     step = 4 if depth % 4 == 0 else depth
-    flat = step * rows * pairs
+    couples = rows // 2
+    flat = step * couples * pairs
     block = 14 * half
     gz, xy = lax.axis_index("gz"), lax.axis_index("xy")
     place, sizes = (gz, xy), (n_gz, n_xy)
@@ -369,7 +373,11 @@
     loads[3].wait()
     mixed = mix[...].astype(F32)
     mixed = jnp.concatenate([mixed, jnp.zeros_like(mixed)], axis=1)
-    mix2 = jnp.concatenate([mixed, pltpu.roll(mixed, half, 1)], axis=0).T.astype(BF16)
+    mix2 = jnp.concatenate([mixed, pltpu.roll(mixed, half, 1)], axis=0).T
+    blank = jnp.zeros_like(mix2)
+    mix4 = jnp.concatenate(
+        [jnp.concatenate([mix2, blank], axis=1), jnp.concatenate([blank, mix2], axis=1)], axis=0
+    ).astype(BF16)
 
     for load in loads[4:]:
         load.wait()
@@ -392,7 +400,9 @@
             start = pl.multiple_of(z * pairs * rows + tile * span, 8)
             tall[pl.ds(start, span), :] = held[tile].reshape(span, lanes)
         for y in range(rows):
-            cot[z, y] = tall[pl.ds(z * pairs * rows + y, pairs, stride=rows), :]
+            cot[lax.div(z, step), y // 2, lax.rem(z, step), :, pl.ds(y % 2 * lanes, lanes)] = tall[
+                pl.ds(z * pairs * rows + y, pairs, stride=rows), :
+            ]
         return carry
 
     lax.fori_loop(0, depth, pick, 0)
@@ -401,30 +411,40 @@
     frame_sides(xw, half)
 
     def put(target, z, cells, period):
-        target[pl.ds(z + 1, step), inner, :, pl.ds(0, lanes)] = cells.astype(BF16)
-        close = cells.astype(F32).reshape(step * rows, pairs, lanes)
-        target[pl.ds(z + 1, step), inner, :, pl.ds(lanes, lanes)] = (
-            side_lanes(close, half, period).astype(BF16).reshape(step, rows, pairs, lanes)
-        )
-
-    brick = (step, rows, pairs, lanes)
+        for y in range(rows):
+            odd, first = y % 2, y // 2 * step * pairs
+            own = cells[first : first + step * pairs, odd * lanes : (odd + 1) * lanes]
+            own = own.reshape(step, pairs, lanes)
+            target[pl.ds(z + 1, step), y + 1, :, pl.ds(0, lanes)] = own
+            target[pl.ds(z + 1, step), y + 1, :, pl.ds(lanes, lanes)] = side_lanes(
+                own.astype(F32), half, period
+            ).astype(BF16)
+
+    def take(framed, z):
+        parts = [framed[pl.ds(z + 1, step), y + 1, :, pl.ds(0, lanes)] for y in range(rows)]
+        parts = [part.reshape(step * pairs, lanes) for part in parts]
+        lines = [jnp.concatenate(parts[odd::2], axis=0) for odd in range(2)]
+        return jnp.concatenate(lines, axis=1).astype(F32)
+
+    def line(z):
+        return pl.ds(z * couples * pairs, flat)
+
     for z in range(0, depth, step):
-        own = xw[pl.ds(z + 1, step), inner, :, pl.ds(0, lanes)].astype(F32).reshape(flat, lanes)
-        feature = (own + conv_rows(xw, wb, z, step)).astype(BF16)
-        put(fw, z, feature.reshape(brick), period)
+        put(fw, z, (take(xw, z) + conv_rows(xw, wb, z, step)).astype(BF16), period)
     for z in range(0, depth, step):
         pre = conv_rows(fw, wr, z, step)
         sig = jax.nn.sigmoid(pre)
-        upstream = cot[pl.ds(z, step)].reshape(flat, lanes).astype(BF16)
-        gate_s[pl.ds(z * rows * pairs, flat), :] = (pre * sig).astype(BF16)
-        gated_grad = jnp.dot(upstream, mix2, preferred_element_type=F32)
+        upstream = cot[z // step].reshape(flat, 2 * lanes).astype(BF16)
+        gate_s[line(z), :] = (pre * sig).astype(BF16)
+        gated_grad = jnp.dot(upstream, mix4, preferred_element_type=F32)
         pre_grad = (gated_grad * sig * (1.0 + pre * (1.0 - sig))).astype(BF16)
-        pg_s[pl.ds(z * rows * pairs, flat), :] = pre_grad
-        put(pw, z, pre_grad.reshape(brick), period)
-
-    outer_sums(sum_a, 0, fw, pg_s[...].T, half)
-    cot_rows = cot[...].reshape(depth * rows * pairs, lanes).astype(BF16)
+        pg_s[line(z), :] = pre_grad
+        put(pw, z, pre_grad, period)
+
+    outer_sums(sum_a, fw, pg_s[...].T, half, step)
+    cot_rows = cot[...].reshape(depth * couples * pairs, 2 * lanes).astype(BF16)
     both = jnp.dot(gate_s[...].T, cot_rows, preferred_element_type=F32)
+    both = both[:lanes, :lanes] + both[lanes:, lanes:]
     lane = lax.broadcasted_iota(jnp.int32, (half, lanes), 1)
     sum_a[pl.ds(block, half), :] = jnp.where(
         lane < half, both[:half] + pltpu.roll(both[half:], half, 1), 0.0
@@ -435,13 +455,13 @@
     total_a.start()
 
     for z in range(0, depth, step):
-        upstream = cot[pl.ds(z, step)].reshape(flat, lanes)
+        upstream = cot[z // step].reshape(flat, 2 * lanes)
         grad = (upstream + conv_rows(pw, wrt, z, step)).astype(BF16)
-        put(gw, z, grad.reshape(brick), pairs)
+        own_s[line(z), :] = grad
+        put(gw, z, grad, pairs)
     grad_rims.start()
 
-    own = gw[pl.ds(1, depth), inner, :, pl.ds(0, lanes)].reshape(depth * rows * pairs, lanes)
-    outer_sums(sum_b, 0, xw, own.T, half)
+    outer_sums(sum_b, xw, own_s[...].T, half, step)
     if block < sum_b.shape[0]:
         sum_b[pl.ds(block, sum_b.shape[0] - block), :] = jnp.zeros((sum_b.shape[0] - block, lanes), BF16)
     total_b.start()
@@ -451,8 +471,13 @@
     frame_sides(gw, half)
 
     def back_conv(z):
-        own = gw[pl.ds(z + 1, step), inner, :, pl.ds(0, lanes)].astype(F32).reshape(flat, lanes)
-        tall[pl.ds(z * rows * pairs, flat), :] = own + conv_rows(gw, wbt, z, step)
+        grad = own_s[line(z), :].astype(F32) + conv_rows(gw, wbt, z, step)
+        grad = grad.reshape(couples, step, pairs, 2 * lanes)
+        for y in range(rows):
+            for level in range(step):
+                tall[pl.ds(((z + level) * rows + y) * pairs, pairs), :] = grad[
+                    y // 2, level, :, y % 2 * lanes : (y % 2 + 1) * lanes
+                ]
 
     back_conv(0)
     total_b.middle()
@@ -463,51 +488,53 @@
     def turn_out(z, carry):
         for pair in range(pairs):
             cells = tall[pl.ds(z * pairs * rows + pair, rows, stride=pairs), :]
-            vout[z, pair] = cells.astype(BF16)
+            vgrad[z, pair] = cells.astype(BF16)
         return carry
 
     lax.fori_loop(0, depth, turn_out, 0)
-    store = pltpu.make_async_copy(vout, vgrad_h, local.at[len(loads)])
-    store.start()
     total_b.spread()
     total_a.finish()
+    write_step(tot_a, refine_step, half)
+    values = tot_a[pl.ds(block, half), :].astype(F32)
+    mix_step[...] = (values / scale_of(values, 1.0 * half * half))[:, :half]
     total_b.finish()
     rims.wait_send()
     grad_rims.wait_send()
     total_a.drain()
     total_b.drain()
-    store.wait()
-
-
-def finish_kernel(tot_a, tot_b, back_step, refine_step, mix_step):
-    half = mix_step.shape[0]
+
+
+def scale_of(values, count):
+    squares = jnp.sum(values * values, axis=0, keepdims=True)
+    return jnp.sqrt(jnp.sum(squares, axis=1, keepdims=True) / count + EPSILON)
+
+
+def write_step(totals, out, half):
     lanes = 2 * half
-    block = 14 * half
-    low = lax.broadcasted_iota(jnp.int32, (half, lanes), 1) < half
-
-    def scale_of(values, count):
-        squares = jnp.sum(values * values, axis=0, keepdims=True)
-        return jnp.sqrt(jnp.sum(squares, axis=1, keepdims=True) / count + EPSILON)
-
-    for totals, out in ((tot_b, back_step), (tot_a, refine_step)):
-        values = totals[pl.ds(0, block), :].astype(F32)
-        scale = scale_of(values, 27.0 * half * half)
-        lows, highs = [None] * 28, [None] * 28
-        for tile in range(14):
-            near = values[tile * half : (tile + 1) * half]
-            both = jnp.concatenate([near, pltpu.roll(near, half, 1)], axis=0).T / scale
-            if tile < 9:
-                first, second = 3 * tile, 3 * tile + 1
-            else:
-                first, second = 6 * (tile - 9) + 2, 6 * (tile - 9) + 5
-            lows[first], highs[first] = both[:half], both[half:]
-            if second < 27:
-                lows[second], highs[second] = both[half:], both[:half]
-        for k in range(0, 26, 2):
-            out[:, pl.ds(k * half, lanes)] = jnp.where(low, lows[k], highs[k + 1])
-        out[:, pl.ds(26 * half, half)] = lows[26][:, :half]
-    values = tot_a[pl.ds(block, half), :].astype(F32)
-    mix_step[...] = (values / scale_of(values, 1.0 * half * half))[:, :half]
+    values = totals[pl.ds(0, 14 * half), :].astype(F32)
+    scale = scale_of(values, 27.0 * half * half)
+    for quad in range(7):
+        turned = values[quad * lanes : (quad + 1) * lanes].T / scale
+        out[:, pl.ds(quad * 2 * lanes, lanes)] = turned[:half]
+        wide = min(lanes, out.shape[1] - quad * 2 * lanes - lanes)
+        out[:, pl.ds(quad * 2 * lanes + lanes, wide)] = turned[half:, :wide]
+
+
+def finish_kernel(
+    vgrad, refine_step, mix_step, tot_b, vgrad_out, back_out, refine_out, mix_out, back_step, sems
+):
+    copies = [
+        pltpu.make_async_copy(source, target, sems.at[number])
+        for number, (source, target) in enumerate(
+            ((vgrad, vgrad_out), (refine_step, refine_out), (mix_step, mix_out), (back_step, back_out))
+        )
+    ]
+    for copy in copies[:3]:
+        copy.start()
+    write_step(tot_b, back_step, mix_step.shape[0])
+    copies[3].start()
+    for copy in copies:
+        copy.wait()
 
 
 def body(volume, backbone_weight, refine_weight, mix_weight, tile_cot, tile_slot, tile_count):
@@ -515,7 +542,7 @@
     channels = mix_weight.shape[0]
     edge = tile_cot.shape[4]
     owners, capacity = tile_cot.shape[2], tile_cot.shape[3]
-    assert depth == edge and rows == edge
+    assert depth == edge and rows == edge and rows % 2 == 0
     lanes = 2 * channels
     pairs = width // lanes
     period = edge // 2
@@ -535,18 +562,23 @@
     chunk_a = -(-(block + channels) // (members * 16)) * 16
     chunk_b = -(-block // (members * 16)) * 16
     framed = pltpu.VMEM((depth + 2, rows + 2, pairs, 2 * lanes), BF16)
-    band = pltpu.VMEM((36 * channels, lanes), BF16)
+    band = pltpu.VMEM((48 * channels, 2 * lanes), BF16)
+    wide = jax.ShapeDtypeStruct((channels, 27 * channels), F32)
+    small = jax.ShapeDtypeStruct((channels, channels), F32)
     cells = depth * rows * pairs
     dma = pltpu.SemaphoreType.DMA
-    vgrad, tot_a, tot_b = pl.pallas_call(
+    step = 4 if depth % 4 == 0 else depth
+    operands = (vol, cot, backbone_weight, refine_weight, mix_weight, slot, count)
+    vgrad, tot_b, refine_step, mix_step = pl.pallas_call(
         functools.partial(step_kernel, n_gz, n_xy, n_x, period),
         out_shape=(
             jax.ShapeDtypeStruct(vol.shape, BF16),
-            jax.ShapeDtypeStruct((members * chunk_a, lanes), BF16),
             jax.ShapeDtypeStruct((members * chunk_b, lanes), BF16),
+            wide,
+            small,
         ),
-        in_specs=[ANY] * 7,
-        out_specs=(ANY, VMEM, VMEM),
+        in_specs=[HBM] * 7,
+        out_specs=(VMEM,) * 4,
         scratch_shapes=[
             pltpu.VMEM(vol.shape, BF16),
             pltpu.VMEM(cot.shape, BF16),
@@ -555,13 +587,14 @@
             pltpu.VMEM(mix_weight.shape, BF16),
             pltpu.SMEM(slot.shape, jnp.int32),
             pltpu.SMEM(count.shape, jnp.int32),
-            pltpu.VMEM(vol.shape, BF16),
             pltpu.VMEM((cells, lanes), F32),
-            pltpu.VMEM((depth, rows, pairs, lanes), F32),
+            pltpu.VMEM((depth // step, rows // 2, step, pairs, 2 * lanes), F32),
             framed, framed, framed, framed,
             band, band, band, band,
-            pltpu.VMEM((cells, lanes), BF16),
-            pltpu.VMEM((cells, lanes), BF16),
+            pltpu.VMEM((cells // 2, 2 * lanes), BF16),
+            pltpu.VMEM((cells // 2, 2 * lanes), BF16),
+            pltpu.VMEM((cells // 2, 2 * lanes), BF16),
+            pltpu.VMEM((members * chunk_a, lanes), BF16),
             pltpu.VMEM((members * chunk_a, lanes), BF16),
             pltpu.VMEM((members * chunk_b, lanes), BF16),
             pltpu.VMEM((members, chunk_a, lanes), BF16),
@@ -573,16 +606,17 @@
         ]
         + [dma((n,)) for n in (members, members, levels, levels, members, members)] * 2,
         compiler_params=pltpu.CompilerParams(
-            collective_id=0, has_side_effects=True, vmem_limit_bytes=56 * 1024 * 1024
+            collective_id=0, has_side_effects=True, vmem_limit_bytes=32 * 1024 * 1024
         ),
-    )(vol, cot, backbone_weight, refine_weight, mix_weight, slot, count)
-    wide = jax.ShapeDtypeStruct((channels, 27 * channels), F32)
-    back_step, refine_step, mix_step = pl.pallas_call(
+    )(*[pltpu.with_memory_space_constraint(operand, pltpu.HBM) for operand in operands])
+    vgrad, back_step, refine_step, mix_step = pl.pallas_call(
         finish_kernel,
-        out_shape=(wide, wide, jax.ShapeDtypeStruct((channels, channels), F32)),
-        in_specs=[VMEM] * 2,
-        out_specs=(VMEM,) * 3,
-    )(tot_a, tot_b)
+        out_shape=(jax.ShapeDtypeStruct(vol.shape, BF16), wide, wide, small),
+        in_specs=[VMEM] * 4,
+        out_specs=(ANY,) * 4,
+        scratch_shapes=[pltpu.VMEM(wide.shape, F32), dma((4,))],
+        compiler_params=pltpu.CompilerParams(vmem_limit_bytes=8 * 1024 * 1024),
+    )(vgrad, refine_step, mix_step, tot_b)
     vgrad = vgrad.transpose(0, 2, 1, 3).reshape(depth, rows, width)
     return (vgrad, back_step, refine_step, mix_step)
 

time: 37.4 us -> 33.9 us (0.906)
  Pallas kernels: 35.8 us -> 33.1 us
  local copies, waits for them, and re-layouts: 0.71 us -> 0 us
    pallas_call x1, Pallas kernels: 2.65 us -> 1.06 us  [body(): pl.pallas_call(finish_kernel, out_shape=(jax.ShapeDtypeStruct(vol.shape,...]
    pallas_call x1, Pallas kernels: 33.2 us -> 32 us  [body(): pl.pallas_call(functools.partial(step_kernel, n_gz, n_xy, n_x, period), o...]
    unnamed x3 -> x0, local copies, waits for them, and re-layouts: 0.71 us -> none
where the time goes in v2:
time: 33.9 us; the launch traced here: 33.7 us
  Pallas kernels  33.1 us (98%)
  between operations  0.64 us (2%)
    pallas_call x1, Pallas kernels, body(): pl.pallas_call(functools.partial(step_kernel, n_gz, n_xy, n_x, period), o...  32 us
    pallas_call x1, Pallas kernels, body(): pl.pallas_call(finish_kernel, out_shape=(jax.ShapeDtypeStruct(vol.shape,...  1.06 us

profile of v2, /device:TPU:0, one launch (start us, length us, event | category | flops | bytes accessed | tf_op | source)
XLA Modules:
  0.0 33.7 jit_solution(363731506610788367)
XLA Ops:
  0.6 32.0 %shard_map.102 = (bf16[8,16,8,128]{3,2,1,0:T(8,128)(2,1)S(1)}, bf16[896,128]{1,0:T(8,128)(2,1)S(1)}, f32[64,1728]{1,0:T(8,128)S(1)}, f32[64,64]{1,0:T(8,128)S(1)}) custom-call(bf16[8,16,8,128]{3,2,1,0:T(8,128)(2,1)} %bitcast.14, bf16[16,8,4,8,128]{4,3,2,1,0:T(8,128)(2,1)} %bitcast.13, bf16[64,1728]{1,0:T(8,128)(2,1)} %back_h.1, bf16[64,1728]{1,0:T(8,128)(2,1)} %refine_h.1, ...), custom_call_target="tpu_custom_call" | custom-call | tf_op jit(solution)/shard_map/pallas_call | solution.py:572
  32.6 1.1 %shard_map.103 = (bf16[8,16,8,128]{3,2,1,0:T(8,128)(2,1)}, f32[64,1728]{1,0:T(8,128)}, f32[64,1728]{1,0:T(8,128)}, f32[64,64]{1,0:T(8,128)}) custom-call(bf16[8,16,8,128]{3,2,1,0:T(8,128)(2,1)S(1)} %get-tuple-element.12.vgrad, f32[64,1728]{1,0:T(8,128)S(1)} %get-tuple-element.13.refine_step, f32[64,64]{1,0:T(8,128)S(1)} %get-tuple-element.14.mix_step, ...), custom_call_target="tpu_custom_call" | custom-call | tf_op jit(solution)/shard_map/pallas_call | solution.py:612

commit v3 on v2

--- a/solution.py
+++ b/solution.py
@@ -77,87 +77,122 @@
 
 
 class Plane:
-    def __init__(self, n_gz, n_xy, n_x):
+    def __init__(self, n_gz, n_xy, n_x, n_core):
         gz, xy = lax.axis_index("gz"), lax.axis_index("xy")
-        self.n_x = n_x
+        self.gz, self.xy, self.n_x, self.n_core = gz, xy, n_x, n_core
         self.members, self.levels = n_gz * n_x, n_xy // n_x
+        self.chips = self.members // n_core
         self.level, self.x = lax.div(xy, n_x), lax.rem(xy, n_x)
+        self.core = lax.rem(gz, n_core)
         self.me = gz * n_x + self.x
-        self.gz = gz
+        self.chip = lax.div(gz, n_core) * n_x + self.x
 
     def member(self, step):
         who = lax.rem(self.me + step, self.members)
         return who, (lax.div(who, self.n_x), self.level * self.n_x + lax.rem(who, self.n_x))
 
+    def other_chip(self, step):
+        who = lax.rem(self.chip + step, self.chips)
+        gz = lax.div(who, self.n_x) * self.n_core + self.core
+        return who, (gz, self.level * self.n_x + lax.rem(who, self.n_x))
+
+    def other_core(self):
+        return self.gz + 1 - 2 * self.core, self.xy
+
     def above(self, step):
         level = lax.rem(self.level + step, self.levels)
         return self.gz, level * self.n_x + self.x
 
 
-def each(count, action):
-    def one(step, carry):
-        action(step)
-        return carry
-
-    lax.fori_loop(1, count, one, 0)
-
-
 class Total:
-    def __init__(self, plane, sums, got, level_got, out, sems):
-        self.plane, self.sums, self.got, self.level_got, self.out = plane, sums, got, level_got, out
-        self.sems = sems
+    def __init__(self, plane, paired, sums, mate, half_sum, got, level_got, out, send, recv):
+        self.plane, self.paired, self.sums, self.mate, self.half_sum = plane, paired, sums, mate, half_sum
+        self.got, self.level_got, self.out, self.send, self.recv = got, level_got, out, send, recv
         self.chunk = got.shape[1]
-        self.own = pl.ds(pl.multiple_of(plane.me * self.chunk, self.chunk), self.chunk)
-
-    def remote(self, stage, step, source, target, device):
+        self.count = plane.chips if paired else plane.members
+        self.span = self.count * self.chunk
+        base = plane.core * self.span if paired else 0
+        self.half = pl.ds(pl.multiple_of(base, self.chunk), self.span)
+        here = plane.chip if paired else plane.me
+        self.mine = pl.ds(pl.multiple_of(here * self.chunk, self.chunk), self.chunk)
+        self.own = pl.ds(pl.multiple_of(base + here * self.chunk, self.chunk), self.chunk)
+
+    def peer(self, step):
+        return self.plane.other_chip(step) if self.paired else self.plane.member(step)
+
+    def remote(self, stage, source, target, device):
         return pltpu.make_async_remote_copy(
             src_ref=source,
             dst_ref=target,
-            send_sem=self.sems[2 * stage].at[step],
-            recv_sem=self.sems[2 * stage + 1].at[step],
+            send_sem=self.send.at[stage],
+            recv_sem=self.recv.at[stage],
             device_id=device,
             device_id_type=MESH,
         )
 
-    def scatter(self, step):
-        who, device = self.plane.member(step)
-        part = pl.ds(pl.multiple_of(who * self.chunk, self.chunk), self.chunk)
-        return self.remote(0, step, self.sums.at[part], self.got.at[step], device)
-
-    def column(self, step):
+    def whole(self, stage):
+        if stage in (0, 4):
+            ref, device = self.mate, self.plane.other_core()
+        elif stage == 2:
+            ref, device = self.level_got.at[pl.ds(0, self.plane.levels - 1)], self.plane.above(1)
+        else:
+            ref, device = self.got, self.peer(1)[1]
+        return self.remote(stage, ref, ref, device)
+
+    def start(self):
+        if self.paired:
+            other = (1 - self.plane.core) * self.span
+            other = pl.ds(pl.multiple_of(other, self.chunk), self.span)
+            self.remote(0, self.sums.at[other], self.mate, self.plane.other_core()).start()
+        else:
+            self.scatter(self.sums)
+
+    def scatter(self, source):
+        for step in range(1, self.count):
+            who, device = self.peer(step)
+            part = pl.ds(pl.multiple_of(who * self.chunk, self.chunk), self.chunk)
+            self.remote(1, source.at[part], self.got.at[step - 1], device).start()
+
+    def pair(self):
+        if self.paired:
+            self.whole(0).wait_recv()
+            total = self.sums[self.half, :].astype(F32) + self.mate[...].astype(F32)
+            self.half_sum[...] = total.astype(BF16)
+            self.scatter(self.half_sum)
+
+    def middle(self):
+        self.whole(1).wait_recv()
+        total = (self.half_sum if self.paired else self.sums)[self.mine, :].astype(F32)
+        for step in range(1, self.count):
+            total = total + self.got[step - 1].astype(F32)
         here = self.level_got.at[self.plane.level]
-        return self.remote(1, step, here, here, self.plane.above(step))
-
-    def gather(self, step):
-        here = self.out.at[self.own]
-        return self.remote(2, step, here, here, self.plane.member(step)[1])
-
-    def start(self):
-        each(self.plane.members, lambda step: self.scatter(step).start())
-
-    def middle(self):
-        each(self.plane.members, lambda step: self.scatter(step).wait_recv())
-        total = self.sums[self.own, :].astype(F32)
-        for step in range(1, self.plane.members):
-            total = total + self.got[step].astype(F32)
         self.level_got[self.plane.level] = total.astype(BF16)
-        each(self.plane.levels, lambda step: self.column(step).start())
+        for step in range(1, self.plane.levels):
+            self.remote(2, here, here, self.plane.above(step)).start()
 
     def spread(self):
-        each(self.plane.levels, lambda step: self.column(step).wait_recv())
+        self.whole(2).wait_recv()
         total = self.level_got[0].astype(F32)
         for level in range(1, self.plane.levels):
             total = total + self.level_got[level].astype(F32)
         self.out[self.own, :] = total.astype(BF16)
-        each(self.plane.members, lambda step: self.gather(step).start())
+        here = self.out.at[self.own]
+        for step in range(1, self.count):
+            self.remote(3, here, here, self.peer(step)[1]).start()
 
     def finish(self):
-        each(self.plane.members, lambda step: self.gather(step).wait_recv())
+        self.whole(3).wait_recv()
+        if self.paired:
+            here = self.out.at[self.half]
+            self.remote(4, here, here, self.plane.other_core()).start()
+
+    def end(self):
+        if self.paired:
+            self.whole(4).wait_recv()
 
     def drain(self):
-        each(self.plane.members, lambda step: self.scatter(step).wait_send())
-        each(self.plane.levels, lambda step: self.column(step).wait_send())
-        each(self.plane.members, lambda step: self.gather(step).wait_send())
+        for stage in (0, 1, 2, 3, 4) if self.paired else (1, 2, 3):
+            self.whole(stage).wait_send()
 
 
 def weight_halves(weight, half, turned):
@@ -228,8 +263,11 @@
     return jnp.dot(jnp.concatenate(parts, axis=1), weight[...], preferred_element_type=F32)
 
 
-def outer_sums(out, windows, grad_turned, half, step):
-    depth = windows.shape[0] - 2
+def outer_sums(out, windows, grads, half):
+    depth, rows, pairs, width = windows.shape
+    inner = (pl.ds(1, depth - 2), pl.ds(1, rows - 2))
+    cells = (depth - 2) * (rows - 2) * pairs
+    grad_turned = grads[inner + (slice(None), pl.ds(0, 2 * half))].reshape(cells, 2 * half).T
     lanes = 2 * half
     low = lax.broadcasted_iota(jnp.int32, (half, lanes), 1) < half
     held = {}
@@ -238,13 +276,9 @@
         return pltpu.roll(values, half, 1)
 
     for dz in range(3):
-        products = []
-        for dy in range(4):
-            seen = [window_rows(windows, z, step, dz, dy) for z in range(0, depth, step)]
-            seen = jnp.concatenate(seen, axis=0)
-            products.append(jnp.dot(grad_turned, seen, preferred_element_type=F32))
         for dy in range(3):
-            both = products[dy][:lanes] + products[dy + 1][lanes:]
+            seen = windows[pl.ds(dz, depth - 2), pl.ds(dy, rows - 2)].reshape(cells, width)
+            both = jnp.dot(grad_turned, seen, preferred_element_type=F32)
             top_near, top_far = both[:half, :lanes], both[:half, lanes:]
             last_near, last_far = both[half:, :lanes], both[half:, lanes:]
             sums = ((top_far, last_near), (last_near, top_near), (top_near, last_far))
@@ -285,13 +319,13 @@
 
 
 def step_kernel(
-    n_gz, n_xy, n_x, period,
+    n_gz, n_xy, n_x, n_core, paired_a, paired_b, period,
     vol_h, cot_h, back_h, refine_h, mix_h, slot_h, count_h,
     vgrad, tot_b, refine_step, mix_step,
     vin, cin, back, refine, mix, slot, count,
-    tall, cot, xw, fw, pw, gw, wb, wr, wrt, wbt, gate_s, pg_s, own_s,
-    tot_a, sum_a, sum_b, got_a, got_b, level_a, level_b,
-    local, rim_send, rim_recv, grad_send, grad_recv, *sems,
+    tall, cot, xw, fw, pw, gw, wb, wr, wrt, wbt, gate_s, own_s,
+    tot_a, sum_a, sum_b, mate_a, mate_b, half_a, half_b, got_a, got_b, level_a, level_b,
+    local, rim_send, rim_recv, grad_send, grad_recv, send_a, recv_a, send_b, recv_b,
 ):
     depth, pairs, rows, lanes = vin.shape
     half = lanes // 2
@@ -303,11 +337,15 @@
     block = 14 * half
     gz, xy = lax.axis_index("gz"), lax.axis_index("xy")
     place, sizes = (gz, xy), (n_gz, n_xy)
-    plane = Plane(n_gz, n_xy, n_x)
+    plane = Plane(n_gz, n_xy, n_x, n_core)
     rims = Rims(sizes, place, xw, depth, rows, lanes, rim_send, rim_recv)
     grad_rims = Rims(sizes, place, gw, depth, rows, lanes, grad_send, grad_recv)
-    total_a = Total(plane, sum_a, got_a, level_a, tot_a, sems[:6])
-    total_b = Total(plane, sum_b, got_b, level_b, tot_b, sems[6:])
+    total_a = Total(
+        plane, paired_a, sum_a, mate_a, half_a, got_a, level_a, tot_a, send_a, recv_a
+    )
+    total_b = Total(
+        plane, paired_b, sum_b, mate_b, half_b, got_b, level_b, tot_b, send_b, recv_b
+    )
 
     loads = [
         pltpu.make_async_copy(source, target, local.at[number])
@@ -335,8 +373,10 @@
         def _():
             greet(where)
 
-    each(plane.members, lambda step: greet(plane.member(step)[1]))
-    each(plane.levels, lambda step: greet(plane.above(step)))
+    for hop in range(1, plane.members):
+        greet(plane.member(hop)[1])
+    for hop in range(1, plane.levels):
+        greet(plane.above(hop))
 
     loads[0].wait()
 
@@ -438,10 +478,9 @@
         gate_s[line(z), :] = (pre * sig).astype(BF16)
         gated_grad = jnp.dot(upstream, mix4, preferred_element_type=F32)
         pre_grad = (gated_grad * sig * (1.0 + pre * (1.0 - sig))).astype(BF16)
-        pg_s[line(z), :] = pre_grad
         put(pw, z, pre_grad, period)
 
-    outer_sums(sum_a, fw, pg_s[...].T, half, step)
+    outer_sums(sum_a, fw, pw, half)
     cot_rows = cot[...].reshape(depth * couples * pairs, 2 * lanes).astype(BF16)
     both = jnp.dot(gate_s[...].T, cot_rows, preferred_element_type=F32)
     both = both[:lanes, :lanes] + both[lanes:, lanes:]
@@ -460,11 +499,13 @@
         own_s[line(z), :] = grad
         put(gw, z, grad, pairs)
     grad_rims.start()
-
-    outer_sums(sum_b, xw, own_s[...].T, half, step)
+    total_a.pair()
+
+    outer_sums(sum_b, xw, gw, half)
     if block < sum_b.shape[0]:
         sum_b[pl.ds(block, sum_b.shape[0] - block), :] = jnp.zeros((sum_b.shape[0] - block, lanes), BF16)
     total_b.start()
+    total_b.pair()
     total_a.middle()
 
     grad_rims.wait_recv()
@@ -494,10 +535,12 @@
     lax.fori_loop(0, depth, turn_out, 0)
     total_b.spread()
     total_a.finish()
+    total_a.end()
     write_step(tot_a, refine_step, half)
     values = tot_a[pl.ds(block, half), :].astype(F32)
     mix_step[...] = (values / scale_of(values, 1.0 * half * half))[:, :half]
     total_b.finish()
+    total_b.end()
     rims.wait_send()
     grad_rims.wait_send()
     total_a.drain()
@@ -552,6 +595,10 @@
     if n_xy % n_x:
         n_x = 1
     members, levels = n_gz * n_x, n_xy // n_x
+    n_core = 2 if n_gz % 2 == 0 else 1
+    paired_a, paired_b = n_core == 2 and True, n_core == 2 and False
+    count_a = members // 2 if paired_a else members
+    count_b = members // 2 if paired_b else members
 
     vol = volume.reshape(depth, rows, pairs, lanes).transpose(0, 2, 1, 3)
     cot = tile_cot.reshape(slots, edge, edge, period, lanes).transpose(0, 1, 3, 2, 4)
@@ -570,7 +617,7 @@
     step = 4 if depth % 4 == 0 else depth
     operands = (vol, cot, backbone_weight, refine_weight, mix_weight, slot, count)
     vgrad, tot_b, refine_step, mix_step = pl.pallas_call(
-        functools.partial(step_kernel, n_gz, n_xy, n_x, period),
+        functools.partial(step_kernel, n_gz, n_xy, n_x, n_core, paired_a, paired_b, period),
         out_shape=(
             jax.ShapeDtypeStruct(vol.shape, BF16),
             jax.ShapeDtypeStruct((members * chunk_b, lanes), BF16),
@@ -593,18 +640,21 @@
             band, band, band, band,
             pltpu.VMEM((cells // 2, 2 * lanes), BF16),
             pltpu.VMEM((cells // 2, 2 * lanes), BF16),
-            pltpu.VMEM((cells // 2, 2 * lanes), BF16),
             pltpu.VMEM((members * chunk_a, lanes), BF16),
             pltpu.VMEM((members * chunk_a, lanes), BF16),
             pltpu.VMEM((members * chunk_b, lanes), BF16),
-            pltpu.VMEM((members, chunk_a, lanes), BF16),
-            pltpu.VMEM((members, chunk_b, lanes), BF16),
+            pltpu.VMEM((count_a * chunk_a, lanes), BF16),
+            pltpu.VMEM((count_b * chunk_b, lanes), BF16),
+            pltpu.VMEM((count_a * chunk_a, lanes), BF16),
+            pltpu.VMEM((count_b * chunk_b, lanes), BF16),
+            pltpu.VMEM((count_a - 1, chunk_a, lanes), BF16),
+            pltpu.VMEM((count_b - 1, chunk_b, lanes), BF16),
             pltpu.VMEM((levels, chunk_a, lanes), BF16),
             pltpu.VMEM((levels, chunk_b, lanes), BF16),
-            dma((8,)),
+            dma((7,)),
             dma((8,)), dma((8,)), dma((8,)), dma((8,)),
-        ]
-        + [dma((n,)) for n in (members, members, levels, levels, members, members)] * 2,
+            dma((5,)), dma((5,)), dma((5,)), dma((5,)),
+        ],
         compiler_params=pltpu.CompilerParams(
             collective_id=0, has_side_effects=True, vmem_limit_bytes=32 * 1024 * 1024
         ),

time: 33.9 us -> 32.4 us (0.956)
  Pallas kernels: 33.1 us -> 31.6 us
    pallas_call x1, Pallas kernels: 32 us -> 30.5 us  [body(): pl.pallas_call(functools.partial(step_kernel, n_gz, n_xy, n_x, n_core, pa...]
where the time goes in v3:
time: 32.4 us; the launch traced here: 32.3 us
  Pallas kernels  31.6 us (98%)
  between operations  0.64 us (2%)
    pallas_call x1, Pallas kernels, body(): pl.pallas_call(functools.partial(step_kernel, n_gz, n_xy, n_x, n_core, pa...  30.5 us
    pallas_call x1, Pallas kernels, body(): pl.pallas_call(finish_kernel, out_shape=(jax.ShapeDtypeStruct(vol.shape,...  1.06 us

profile of v3, /device:TPU:0, one launch (start us, length us, event | category | flops | bytes accessed | tf_op | source)
XLA Modules:
  0.0 32.3 jit_solution(15996084822532893374)
XLA Ops:
  0.6 30.5 %shard_map.102 = (bf16[8,16,8,128]{3,2,1,0:T(8,128)(2,1)S(1)}, bf16[896,128]{1,0:T(8,128)(2,1)S(1)}, f32[64,1728]{1,0:T(8,128)S(1)}, f32[64,64]{1,0:T(8,128)S(1)}) custom-call(bf16[8,16,8,128]{3,2,1,0:T(8,128)(2,1)} %bitcast.14, bf16[16,8,4,8,128]{4,3,2,1,0:T(8,128)(2,1)} %bitcast.13, bf16[64,1728]{1,0:T(8,128)(2,1)} %back_h.1, bf16[64,1728]{1,0:T(8,128)(2,1)} %refine_h.1, ...), custom_call_target="tpu_custom_call" | custom-call | tf_op jit(solution)/shard_map/pallas_call | solution.py:619
  31.2 1.1 %shard_map.103 = (bf16[8,16,8,128]{3,2,1,0:T(8,128)(2,1)}, f32[64,1728]{1,0:T(8,128)}, f32[64,1728]{1,0:T(8,128)}, f32[64,64]{1,0:T(8,128)}) custom-call(bf16[8,16,8,128]{3,2,1,0:T(8,128)(2,1)S(1)} %get-tuple-element.12.vgrad, f32[64,1728]{1,0:T(8,128)S(1)} %get-tuple-element.13.refine_step, f32[64,64]{1,0:T(8,128)S(1)} %get-tuple-element.14.mix_step, ...), custom_call_target="tpu_custom_call" | custom-call | tf_op jit(solution)/shard_map/pallas_call | solution.py:662

commit v4 on v3

--- a/solution.py
+++ b/solution.py
@@ -84,12 +84,14 @@
         self.chips = self.members // n_core
         self.level, self.x = lax.div(xy, n_x), lax.rem(xy, n_x)
         self.core = lax.rem(gz, n_core)
-        self.me = gz * n_x + self.x
         self.chip = lax.div(gz, n_core) * n_x + self.x
+        self.me = self.core * self.chips + self.chip
 
     def member(self, step):
         who = lax.rem(self.me + step, self.members)
-        return who, (lax.div(who, self.n_x), self.level * self.n_x + lax.rem(who, self.n_x))
+        core, chip = lax.div(who, self.chips), lax.rem(who, self.chips)
+        gz = lax.div(chip, self.n_x) * self.n_core + core
+        return who, (gz, self.level * self.n_x + lax.rem(chip, self.n_x))
 
     def other_chip(self, step):
         who = lax.rem(self.chip + step, self.chips)
@@ -105,17 +107,19 @@
 
 
 class Total:
-    def __init__(self, plane, paired, sums, mate, half_sum, got, level_got, out, send, recv):
+    def __init__(self, plane, paired, joined, out, sums, mate, half_sum, got, level_got, send, recv):
+        self.joined = joined
         self.plane, self.paired, self.sums, self.mate, self.half_sum = plane, paired, sums, mate, half_sum
         self.got, self.level_got, self.out, self.send, self.recv = got, level_got, out, send, recv
         self.chunk = got.shape[1]
         self.count = plane.chips if paired else plane.members
         self.span = self.count * self.chunk
-        base = plane.core * self.span if paired else 0
-        self.half = pl.ds(pl.multiple_of(base, self.chunk), self.span)
+        base = plane.core * plane.chips * self.chunk
+        self.half = pl.ds(pl.multiple_of(base, self.chunk), plane.chips * self.chunk)
         here = plane.chip if paired else plane.me
         self.mine = pl.ds(pl.multiple_of(here * self.chunk, self.chunk), self.chunk)
-        self.own = pl.ds(pl.multiple_of(base + here * self.chunk, self.chunk), self.chunk)
+        self.own = pl.ds(pl.multiple_of(plane.me * self.chunk, self.chunk), self.chunk)
+        self.readers = plane.chips if joined else plane.members
 
     def peer(self, step):
         return self.plane.other_chip(step) if self.paired else self.plane.member(step)
@@ -131,8 +135,13 @@
         )
 
     def whole(self, stage):
-        if stage in (0, 4):
+        if stage == 0:
             ref, device = self.mate, self.plane.other_core()
+        elif stage == 4:
+            ref, device = self.out.at[self.half], self.plane.other_core()
+        elif stage == 3:
+            ref = self.out.at[pl.ds(0, (self.readers - 1) * self.chunk)]
+            device = self.plane.member(1)[1]
         elif stage == 2:
             ref, device = self.level_got.at[pl.ds(0, self.plane.levels - 1)], self.plane.above(1)
         else:
@@ -177,21 +186,22 @@
             total = total + self.level_got[level].astype(F32)
         self.out[self.own, :] = total.astype(BF16)
         here = self.out.at[self.own]
-        for step in range(1, self.count):
-            self.remote(3, here, here, self.peer(step)[1]).start()
+        for step in range(1, self.readers):
+            reader = self.plane.other_chip(step) if self.joined else self.plane.member(step)
+            self.remote(3, here, here, reader[1]).start()
 
     def finish(self):
         self.whole(3).wait_recv()
-        if self.paired:
+        if self.joined:
             here = self.out.at[self.half]
             self.remote(4, here, here, self.plane.other_core()).start()
 
     def end(self):
-        if self.paired:
+        if self.joined:
             self.whole(4).wait_recv()
 
     def drain(self):
-        for stage in (0, 1, 2, 3, 4) if self.paired else (1, 2, 3):
+        for stage in [0] * self.paired + [1, 2, 3] + [4] * self.joined:
             self.whole(stage).wait_send()
 
 
@@ -263,7 +273,7 @@
     return jnp.dot(jnp.concatenate(parts, axis=1), weight[...], preferred_element_type=F32)
 
 
-def outer_sums(out, windows, grads, half):
+def outer_sums(parts, split, hook, windows, grads, half):
     depth, rows, pairs, width = windows.shape
     inner = (pl.ds(1, depth - 2), pl.ds(1, rows - 2))
     cells = (depth - 2) * (rows - 2) * pairs
@@ -271,6 +281,10 @@
     lanes = 2 * half
     low = lax.broadcasted_iota(jnp.int32, (half, lanes), 1) < half
     held = {}
+
+    def put(tile, values):
+        part, first = (parts[0], 0) if tile < split else (parts[1], split)
+        part[pl.ds((tile - first) * half, half), :] = values.astype(BF16)
 
     def turn(values):
         return pltpu.roll(values, half, 1)
@@ -289,9 +303,11 @@
                     held[tile] = turn(right) + left
                 else:
                     pair = jnp.where(low, held.pop(tile), right + turn(left))
-                    out[pl.ds(tile * half, half), :] = pair.astype(BF16)
+                    put(tile, pair)
+                    if tile == split - 1:
+                        hook()
     for tile, values in held.items():
-        out[pl.ds(tile * half, half), :] = jnp.where(low, values, 0.0).astype(BF16)
+        put(tile, jnp.where(low, values, 0.0))
 
 
 def clear_frame(framed):
@@ -319,13 +335,13 @@
 
 
 def step_kernel(
-    n_gz, n_xy, n_x, n_core, paired_a, paired_b, period,
+    n_gz, n_xy, n_x, n_core, paired, joined, period,
     vol_h, cot_h, back_h, refine_h, mix_h, slot_h, count_h,
-    vgrad, tot_b, refine_step, mix_step,
+    vgrad, tot_2, tot_3, refine_step, mix_step,
     vin, cin, back, refine, mix, slot, count,
     tall, cot, xw, fw, pw, gw, wb, wr, wrt, wbt, gate_s, own_s,
-    tot_a, sum_a, sum_b, mate_a, mate_b, half_a, half_b, got_a, got_b, level_a, level_b,
-    local, rim_send, rim_recv, grad_send, grad_recv, send_a, recv_a, send_b, recv_b,
+    tot_0, tot_1,
+    local, rim_send, rim_recv, grad_recv, *pieces,
 ):
     depth, pairs, rows, lanes = vin.shape
     half = lanes // 2
@@ -334,18 +350,15 @@
     step = 4 if depth % 4 == 0 else depth
     couples = rows // 2
     flat = step * couples * pairs
-    block = 14 * half
+    split = 8
     gz, xy = lax.axis_index("gz"), lax.axis_index("xy")
     place, sizes = (gz, xy), (n_gz, n_xy)
     plane = Plane(n_gz, n_xy, n_x, n_core)
     rims = Rims(sizes, place, xw, depth, rows, lanes, rim_send, rim_recv)
-    grad_rims = Rims(sizes, place, gw, depth, rows, lanes, grad_send, grad_recv)
-    total_a = Total(
-        plane, paired_a, sum_a, mate_a, half_a, got_a, level_a, tot_a, send_a, recv_a
-    )
-    total_b = Total(
-        plane, paired_b, sum_b, mate_b, half_b, got_b, level_b, tot_b, send_b, recv_b
-    )
+    grad_rims = Rims(sizes, place, gw, depth, rows, lanes, rim_send, grad_recv)
+    totals = []
+    for number, tot in enumerate((tot_0, tot_1, tot_2, tot_3)):
+        totals.append(Total(plane, paired[number], joined[number], tot, *pieces[7 * number : 7 * number + 7]))
 
     loads = [
         pltpu.make_async_copy(source, target, local.at[number])
@@ -480,33 +493,41 @@
         pre_grad = (gated_grad * sig * (1.0 + pre * (1.0 - sig))).astype(BF16)
         put(pw, z, pre_grad, period)
 
-    outer_sums(sum_a, fw, pw, half)
+    def begin(number):
+        part = totals[number].sums
+        used = (split if number % 2 == 0 else 15 - split if number == 1 else 14 - split) * half
+        if used < part.shape[0]:
+            part[pl.ds(used, part.shape[0] - used), :] = jnp.zeros((part.shape[0] - used, lanes), BF16)
+        totals[number].start()
+
+    outer_sums((totals[0].sums, totals[1].sums), split, lambda: begin(0), fw, pw, half)
     cot_rows = cot[...].reshape(depth * couples * pairs, 2 * lanes).astype(BF16)
     both = jnp.dot(gate_s[...].T, cot_rows, preferred_element_type=F32)
     both = both[:lanes, :lanes] + both[lanes:, lanes:]
     lane = lax.broadcasted_iota(jnp.int32, (half, lanes), 1)
-    sum_a[pl.ds(block, half), :] = jnp.where(
+    totals[1].sums[pl.ds((14 - split) * half, half), :] = jnp.where(
         lane < half, both[:half] + pltpu.roll(both[half:], half, 1), 0.0
     ).astype(BF16)
-    used = block + half
-    if used < sum_a.shape[0]:
-        sum_a[pl.ds(used, sum_a.shape[0] - used), :] = jnp.zeros((sum_a.shape[0] - used, lanes), BF16)
-    total_a.start()
+    begin(1)
 
     for z in range(0, depth, step):
         upstream = cot[z // step].reshape(flat, 2 * lanes)
         grad = (upstream + conv_rows(pw, wrt, z, step)).astype(BF16)
         own_s[line(z), :] = grad
         put(gw, z, grad, pairs)
+    for total in totals[:2]:
+        total.pair()
+
+    outer_sums((totals[2].sums, totals[3].sums), split, lambda: begin(2), xw, gw, half)
+    begin(3)
+    rims.wait_send()
     grad_rims.start()
-    total_a.pair()
-
-    outer_sums(sum_b, xw, gw, half)
-    if block < sum_b.shape[0]:
-        sum_b[pl.ds(block, sum_b.shape[0] - block), :] = jnp.zeros((sum_b.shape[0] - block, lanes), BF16)
-    total_b.start()
-    total_b.pair()
-    total_a.middle()
+    for total in totals[2:]:
+        total.pair()
+    for total in totals[:2]:
+        total.middle()
+    for total in totals[2:]:
+        total.middle()
 
     grad_rims.wait_recv()
     frame_sides(gw, half)
@@ -521,10 +542,10 @@
                 ]
 
     back_conv(0)
-    total_b.middle()
+    for total in totals[:2]:
+        total.spread()
     for z in range(step, depth, step):
         back_conv(z)
-    total_a.spread()
 
     def turn_out(z, carry):
         for pair in range(pairs):
@@ -533,18 +554,22 @@
         return carry
 
     lax.fori_loop(0, depth, turn_out, 0)
-    total_b.spread()
-    total_a.finish()
-    total_a.end()
-    write_step(tot_a, refine_step, half)
-    values = tot_a[pl.ds(block, half), :].astype(F32)
+    for total in totals[2:]:
+        total.spread()
+    for total in totals[:2]:
+        total.finish()
+    for total in totals[:2]:
+        total.end()
+    write_step(tot_0, tot_1, split, refine_step, half)
+    values = tot_1[pl.ds((14 - split) * half, half), :].astype(F32)
     mix_step[...] = (values / scale_of(values, 1.0 * half * half))[:, :half]
-    total_b.finish()
-    total_b.end()
-    rims.wait_send()
+    for total in totals[2:]:
+        total.finish()
+    for total in totals[2:]:
+        total.end()
     grad_rims.wait_send()
-    total_a.drain()
-    total_b.drain()
+    for total in totals:
+        total.drain()
 
 
 def scale_of(values, count):
@@ -552,9 +577,11 @@
     return jnp.sqrt(jnp.sum(squares, axis=1, keepdims=True) / count + EPSILON)
 
 
-def write_step(totals, out, half):
+def write_step(first, second, split, out, half):
     lanes = 2 * half
-    values = totals[pl.ds(0, 14 * half), :].astype(F32)
+    values = jnp.concatenate(
+        [first[pl.ds(0, split * half), :], second[pl.ds(0, (14 - split) * half), :]], axis=0
+    ).astype(F32)
     scale = scale_of(values, 27.0 * half * half)
     for quad in range(7):
         turned = values[quad * lanes : (quad + 1) * lanes].T / scale
@@ -564,7 +591,7 @@
 
 
 def finish_kernel(
-    vgrad, refine_step, mix_step, tot_b, vgrad_out, back_out, refine_out, mix_out, back_step, sems
+    vgrad, refine_step, mix_step, tot_2, tot_3, vgrad_out, back_out, refine_out, mix_out, back_step, sems
 ):
     copies = [
         pltpu.make_async_copy(source, target, sems.at[number])
@@ -574,7 +601,7 @@
     ]
     for copy in copies[:3]:
         copy.start()
-    write_step(tot_b, back_step, mix_step.shape[0])
+    write_step(tot_2, tot_3, 8, back_step, mix_step.shape[0])
     copies[3].start()
     for copy in copies:
         copy.wait()
@@ -596,18 +623,18 @@
         n_x = 1
     members, levels = n_gz * n_x, n_xy // n_x
     n_core = 2 if n_gz % 2 == 0 else 1
-    paired_a, paired_b = n_core == 2 and True, n_core == 2 and False
-    count_a = members // 2 if paired_a else members
-    count_b = members // 2 if paired_b else members
+    paired = [n_core == 2 and wanted for wanted in (False, False, True, True)]
+    joined = [n_core == 2 and wanted for wanted in (True, True, False, False)]
 
     vol = volume.reshape(depth, rows, pairs, lanes).transpose(0, 2, 1, 3)
     cot = tile_cot.reshape(slots, edge, edge, period, lanes).transpose(0, 1, 3, 2, 4)
     slot = tile_slot.reshape(owners, capacity).T
     count = tile_count.reshape(owners, owners)
 
-    block = 14 * channels
-    chunk_a = -(-(block + channels) // (members * 16)) * 16
-    chunk_b = -(-block // (members * 16)) * 16
+    chunks, counts = [], []
+    for number, tiles in enumerate((8, 7, 8, 6)):
+        counts.append(members // 2 if paired[number] else members)
+        chunks.append(-(-tiles * channels // (members * 16)) * 16)
     framed = pltpu.VMEM((depth + 2, rows + 2, pairs, 2 * lanes), BF16)
     band = pltpu.VMEM((48 * channels, 2 * lanes), BF16)
     wide = jax.ShapeDtypeStruct((channels, 27 * channels), F32)
@@ -616,16 +643,29 @@
     dma = pltpu.SemaphoreType.DMA
     step = 4 if depth % 4 == 0 else depth
     operands = (vol, cot, backbone_weight, refine_weight, mix_weight, slot, count)
-    vgrad, tot_b, refine_step, mix_step = pl.pallas_call(
-        functools.partial(step_kernel, n_gz, n_xy, n_x, n_core, paired_a, paired_b, period),
+    sums = [pltpu.VMEM((members * chunk, lanes), BF16) for chunk in chunks]
+    pieces = []
+    for number, (chunk, peers) in enumerate(zip(chunks, counts)):
+        pieces += [
+            sums[number],
+            pltpu.VMEM((peers * chunk, lanes), BF16),
+            pltpu.VMEM((peers * chunk, lanes), BF16),
+            pltpu.VMEM((peers - 1, chunk, lanes), BF16),
+            pltpu.VMEM((levels, chunk, lanes), BF16),
+            dma((5,)),
+            dma((5,)),
+        ]
+    vgrad, tot_2, tot_3, refine_step, mix_step = pl.pallas_call(
+        functools.partial(step_kernel, n_gz, n_xy, n_x, n_core, paired, joined, period),
         out_shape=(
             jax.ShapeDtypeStruct(vol.shape, BF16),
-            jax.ShapeDtypeStruct((members * chunk_b, lanes), BF16),
+            jax.ShapeDtypeStruct((members * chunks[2], lanes), BF16),
+            jax.ShapeDtypeStruct((members * chunks[3], lanes), BF16),
             wide,
             small,
         ),
         in_specs=[HBM] * 7,
-        out_specs=(VMEM,) * 4,
+        out_specs=(VMEM,) * 5,
         scratch_shapes=[
             pltpu.VMEM(vol.shape, BF16),
             pltpu.VMEM(cot.shape, BF16),
@@ -640,21 +680,12 @@
             band, band, band, band,
             pltpu.VMEM((cells // 2, 2 * lanes), BF16),
             pltpu.VMEM((cells // 2, 2 * lanes), BF16),
-            pltpu.VMEM((members * chunk_a, lanes), BF16),
-            pltpu.VMEM((members * chunk_a, lanes), BF16),
-            pltpu.VMEM((members * chunk_b, lanes), BF16),
-            pltpu.VMEM((count_a * chunk_a, lanes), BF16),
-            pltpu.VMEM((count_b * chunk_b, lanes), BF16),
-            pltpu.VMEM((count_a * chunk_a, lanes), BF16),
-            pltpu.VMEM((count_b * chunk_b, lanes), BF16),
-            pltpu.VMEM((count_a - 1, chunk_a, lanes), BF16),
-            pltpu.VMEM((count_b - 1, chunk_b, lanes), BF16),
-            pltpu.VMEM((levels, chunk_a, lanes), BF16),
-            pltpu.VMEM((levels, chunk_b, lanes), BF16),
+            sums[0],
+            sums[1],
             dma((7,)),
-            dma((8,)), dma((8,)), dma((8,)), dma((8,)),
-            dma((5,)), dma((5,)), dma((5,)), dma((5,)),
-        ],
+            dma((8,)), dma((8,)), dma((8,)),
+        ]
+        + pieces,
         compiler_params=pltpu.CompilerParams(
             collective_id=0, has_side_effects=True, vmem_limit_bytes=32 * 1024 * 1024
         ),
@@ -662,11 +693,11 @@
     vgrad, back_step, refine_step, mix_step = pl.pallas_call(
         finish_kernel,
         out_shape=(jax.ShapeDtypeStruct(vol.shape, BF16), wide, wide, small),
-        in_specs=[VMEM] * 4,
+        in_specs=[VMEM] * 5,
         out_specs=(ANY,) * 4,
         scratch_shapes=[pltpu.VMEM(wide.shape, F32), dma((4,))],
         compiler_params=pltpu.CompilerParams(vmem_limit_bytes=8 * 1024 * 1024),
-    )(vgrad, refine_step, mix_step, tot_b)
+    )(vgrad, refine_step, mix_step, tot_2, tot_3)
     vgrad = vgrad.transpose(0, 2, 1, 3).reshape(depth, rows, width)
     return (vgrad, back_step, refine_step, mix_step)
 

time: 32.4 us -> 29.9 us (0.923)
  Pallas kernels: 31.6 us -> 29.1 us
    pallas_call x1, Pallas kernels: 30.5 us -> 28 us  [body(): pl.pallas_call(functools.partial(step_kernel, n_gz, n_xy, n_x, n_core, pa...]
where the time goes in v4:
time: 29.9 us; the launch traced here: 29.7 us
  Pallas kernels  29.1 us (97%)
  between operations  0.64 us (2%)
    pallas_call x1, Pallas kernels, body(): pl.pallas_call(functools.partial(step_kernel, n_gz, n_xy, n_x, n_core, pa...  28 us
    pallas_call x1, Pallas kernels, body(): pl.pallas_call(finish_kernel, out_shape=(jax.ShapeDtypeStruct(vol.shape,...  1.07 us

profile of v4, /device:TPU:0, one launch (start us, length us, event | category | flops | bytes accessed | tf_op | source)
XLA Modules:
  0.0 29.7 jit_solution(7866666339400701891)
XLA Ops:
  0.6 28.0 %shard_map.102 = (bf16[8,16,8,128]{3,2,1,0:T(8,128)(2,1)S(1)}, bf16[512,128]{1,0:T(8,128)(2,1)S(1)}, bf16[384,128]{1,0:T(8,128)(2,1)S(1)}, f32[64,1728]{1,0:T(8,128)S(1)}, f32[64,64]{1,0:T(8,128)S(1)}) custom-call(bf16[8,16,8,128]{3,2,1,0:T(8,128)(2,1)} %bitcast.14, bf16[16,8,4,8,128]{4,3,2,1,0:T(8,128)(2,1)} %bitcast.13, bf16[64,1728]{1,0:T(8,128)(2,1)} %back_h.1, ...), custom_call_target="tpu_custom_call" | custom-call | tf_op jit(solution)/shard_map/pallas_call | solution.py:658
  28.7 1.1 %shard_map.103 = (bf16[8,16,8,128]{3,2,1,0:T(8,128)(2,1)}, f32[64,1728]{1,0:T(8,128)}, f32[64,1728]{1,0:T(8,128)}, f32[64,64]{1,0:T(8,128)}) custom-call(bf16[8,16,8,128]{3,2,1,0:T(8,128)(2,1)S(1)} %get-tuple-element.13.vgrad, f32[64,1728]{1,0:T(8,128)S(1)} %get-tuple-element.14.refine_step, f32[64,64]{1,0:T(8,128)S(1)} %get-tuple-element.15.mix_step, ...), custom_call_target="tpu_custom_call" | custom-call | tf_op jit(solution)/shard_map/pallas_call | solution.py:693

commit v5 on v4

--- a/solution.py
+++ b/solution.py
@@ -106,9 +106,14 @@
         return self.gz, level * self.n_x + self.x
 
 
+def stages_of(paired, joined):
+    return [0] * paired + [1, 2, 3] + [4] * joined
+
+
 class Total:
     def __init__(self, plane, paired, joined, out, sums, mate, half_sum, got, level_got, send, recv):
         self.joined = joined
+        self.stages = stages_of(paired, joined)
         self.plane, self.paired, self.sums, self.mate, self.half_sum = plane, paired, sums, mate, half_sum
         self.got, self.level_got, self.out, self.send, self.recv = got, level_got, out, send, recv
         self.chunk = got.shape[1]
@@ -128,8 +133,8 @@
         return pltpu.make_async_remote_copy(
             src_ref=source,
             dst_ref=target,
-            send_sem=self.send.at[stage],
-            recv_sem=self.recv.at[stage],
+            send_sem=self.send.at[self.stages.index(stage)],
+            recv_sem=self.recv.at[self.stages.index(stage)],
             device_id=device,
             device_id_type=MESH,
         )
@@ -201,7 +206,7 @@
             self.whole(4).wait_recv()
 
     def drain(self):
-        for stage in [0] * self.paired + [1, 2, 3] + [4] * self.joined:
+        for stage in self.stages:
             self.whole(stage).wait_send()
 
 
@@ -422,7 +427,6 @@
     loads[2].wait()
     fill_band(wr, refine, False)
     fill_band(wrt, refine, True)
-    fill_band(wbt, back, True)
     loads[3].wait()
     mixed = mix[...].astype(F32)
     mixed = jnp.concatenate([mixed, jnp.zeros_like(mixed)], axis=1)
@@ -521,16 +525,6 @@
     outer_sums((totals[2].sums, totals[3].sums), split, lambda: begin(2), xw, gw, half)
     begin(3)
     rims.wait_send()
-    grad_rims.start()
-    for total in totals[2:]:
-        total.pair()
-    for total in totals[:2]:
-        total.middle()
-    for total in totals[2:]:
-        total.middle()
-
-    grad_rims.wait_recv()
-    frame_sides(gw, half)
 
     def back_conv(z):
         grad = own_s[line(z), :].astype(F32) + conv_rows(gw, wbt, z, step)
@@ -541,18 +535,27 @@
                     y // 2, level, :, y % 2 * lanes : (y % 2 + 1) * lanes
                 ]
 
-    back_conv(0)
-    for total in totals[:2]:
-        total.spread()
-    for z in range(step, depth, step):
-        back_conv(z)
-
     def turn_out(z, carry):
         for pair in range(pairs):
             cells = tall[pl.ds(z * pairs * rows + pair, rows, stride=pairs), :]
             vgrad[z, pair] = cells.astype(BF16)
         return carry
 
+    grad_rims.start()
+    fill_band(wbt, back, True)
+    for total in totals[2:]:
+        total.pair()
+    for total in totals[:2]:
+        total.middle()
+    for total in totals[2:]:
+        total.middle()
+    for total in totals[:2]:
+        total.spread()
+    grad_rims.wait_recv()
+    frame_sides(gw, half)
+    back_conv(0)
+    for z in range(step, depth, step):
+        back_conv(z)
     lax.fori_loop(0, depth, turn_out, 0)
     for total in totals[2:]:
         total.spread()
@@ -652,8 +655,8 @@
             pltpu.VMEM((peers * chunk, lanes), BF16),
             pltpu.VMEM((peers - 1, chunk, lanes), BF16),
             pltpu.VMEM((levels, chunk, lanes), BF16),
-            dma((5,)),
-            dma((5,)),
+            dma((len(stages_of(paired[number], joined[number])),)),
+            dma((len(stages_of(paired[number], joined[number])),)),
         ]
     vgrad, tot_2, tot_3, refine_step, mix_step = pl.pallas_call(
         functools.partial(step_kernel, n_gz, n_xy, n_x, n_core, paired, joined, period),

time: 29.9 us -> 29.8 us (level)
  no operation moved by 1% of the time
where the time goes in v5:
time: 29.8 us; the launch traced here: 29.6 us
  Pallas kernels  29 us (97%)
  between operations  0.64 us (2%)
    pallas_call x1, Pallas kernels, body(): pl.pallas_call(functools.partial(step_kernel, n_gz, n_xy, n_x, n_core, pa...  27.9 us
    pallas_call x1, Pallas kernels, body(): pl.pallas_call(finish_kernel, out_shape=(jax.ShapeDtypeStruct(vol.shape,...  1.07 us

profile of v5, /device:TPU:0, one launch (start us, length us, event | category | flops | bytes accessed | tf_op | source)
XLA Modules:
  0.0 29.6 jit_solution(92552233183397756)
XLA Ops:
  0.6 27.9 %shard_map.102 = (bf16[8,16,8,128]{3,2,1,0:T(8,128)(2,1)S(1)}, bf16[512,128]{1,0:T(8,128)(2,1)S(1)}, bf16[384,128]{1,0:T(8,128)(2,1)S(1)}, f32[64,1728]{1,0:T(8,128)S(1)}, f32[64,64]{1,0:T(8,128)S(1)}) custom-call(bf16[8,16,8,128]{3,2,1,0:T(8,128)(2,1)} %bitcast.14, bf16[16,8,4,8,128]{4,3,2,1,0:T(8,128)(2,1)} %bitcast.13, bf16[64,1728]{1,0:T(8,128)(2,1)} %back_h.1, ...), custom_call_target="tpu_custom_call" | custom-call | tf_op jit(solution)/shard_map/pallas_call | solution.py:661
  28.6 1.1 %shard_map.103 = (bf16[8,16,8,128]{3,2,1,0:T(8,128)(2,1)}, f32[64,1728]{1,0:T(8,128)}, f32[64,1728]{1,0:T(8,128)}, f32[64,64]{1,0:T(8,128)}) custom-call(bf16[8,16,8,128]{3,2,1,0:T(8,128)(2,1)S(1)} %get-tuple-element.13.vgrad, f32[64,1728]{1,0:T(8,128)S(1)} %get-tuple-element.14.refine_step, f32[64,64]{1,0:T(8,128)S(1)} %get-tuple-element.15.mix_step, ...), custom_call_target="tpu_custom_call" | custom-call | tf_op jit(solution)/shard_map/pallas_call | solution.py:696

commit v6 on v5

--- a/solution.py
+++ b/solution.py
@@ -585,9 +585,9 @@
     values = jnp.concatenate(
         [first[pl.ds(0, split * half), :], second[pl.ds(0, (14 - split) * half), :]], axis=0
     ).astype(F32)
-    scale = scale_of(values, 27.0 * half * half)
+    scale = 1.0 / scale_of(values, 27.0 * half * half)
     for quad in range(7):
-        turned = values[quad * lanes : (quad + 1) * lanes].T / scale
+        turned = values[quad * lanes : (quad + 1) * lanes].T * scale
         out[:, pl.ds(quad * 2 * lanes, lanes)] = turned[:half]
         wide = min(lanes, out.shape[1] - quad * 2 * lanes - lanes)
         out[:, pl.ds(quad * 2 * lanes + lanes, wide)] = turned[half:, :wide]

time: 29.8 us -> 29.8 us (level)
  no operation moved by 1% of the time
where the time goes in v6:
time: 29.8 us; the launch traced here: 29.6 us
  Pallas kernels  29 us (97%)
  between operations  0.64 us (2%)
    pallas_call x1, Pallas kernels, body(): pl.pallas_call(functools.partial(step_kernel, n_gz, n_xy, n_x, n_core, pa...  27.9 us
    pallas_call x1, Pallas kernels, body(): pl.pallas_call(finish_kernel, out_shape=(jax.ShapeDtypeStruct(vol.shape,...  1.07 us

profile of v6, /device:TPU:0, one launch (start us, length us, event | category | flops | bytes accessed | tf_op | source)
XLA Modules:
  0.0 29.6 jit_solution(92552233183397756)
XLA Ops:
  0.6 27.9 %shard_map.102 = (bf16[8,16,8,128]{3,2,1,0:T(8,128)(2,1)S(1)}, bf16[512,128]{1,0:T(8,128)(2,1)S(1)}, bf16[384,128]{1,0:T(8,128)(2,1)S(1)}, f32[64,1728]{1,0:T(8,128)S(1)}, f32[64,64]{1,0:T(8,128)S(1)}) custom-call(bf16[8,16,8,128]{3,2,1,0:T(8,128)(2,1)} %bitcast.14, bf16[16,8,4,8,128]{4,3,2,1,0:T(8,128)(2,1)} %bitcast.13, bf16[64,1728]{1,0:T(8,128)(2,1)} %back_h.1, ...), custom_call_target="tpu_custom_call" | custom-call | tf_op jit(solution)/shard_map/pallas_call | solution.py:661
  28.6 1.1 %shard_map.103 = (bf16[8,16,8,128]{3,2,1,0:T(8,128)(2,1)}, f32[64,1728]{1,0:T(8,128)}, f32[64,1728]{1,0:T(8,128)}, f32[64,64]{1,0:T(8,128)}) custom-call(bf16[8,16,8,128]{3,2,1,0:T(8,128)(2,1)S(1)} %get-tuple-element.13.vgrad, f32[64,1728]{1,0:T(8,128)S(1)} %get-tuple-element.14.refine_step, f32[64,64]{1,0:T(8,128)S(1)} %get-tuple-element.15.mix_step, ...), custom_call_target="tpu_custom_call" | custom-call | tf_op jit(solution)/shard_map/pallas_call | solution.py:696
